TPU v7x, 32 devices: a whole 2x2x4 slice. The times are simulated.
32 devices in a mesh: rep: 4 (over y, core), shard: 8 (over z, x).
Axes of the slice: x: 2, y: 2, z: 4, core: 2. Of those that a mesh axis runs over, the one named last changes fastest.
Arguments:
- grad_kv: bfloat16 [4, 2, 8192, 1024], P('rep', None, 'shard'), may hold values from -24 to 24
- error_kv: float32 [4, 2, 8192, 1024], P('rep', None, 'shard'), may hold values from -12 to 12
- basis_kv: float32 [2, 1024, 64], replicated, may hold values from -6 to 6
Outputs:
- update_kv: bfloat16 [2, 8192, 1024], P(None, 'shard')
- new_error: float32 [4, 2, 8192, 1024], P('rep', None, 'shard')
- basis_next: float32 [2, 1024, 64], replicated
All inputs are finite; a program needn't handle non-finite values.
Results may differ from a plain program's by a relative error of at most 0.001.
Values sent between devices are 32-bit elements; how exact they have to be, the bound alone decides.
No kernel may reach another device: no remote copies, remote signals or barrier semaphores. Data moves between devices by JAX's collectives and lax.ppermute only.
A program may use at most 64 MiB of HBM per device.

v0:
```python
import functools

import jax
import jax.numpy as jnp
from jax import lax
from jax.experimental import pallas as pl
from jax.experimental.pallas import tpu as pltpu
from jax.sharding import PartitionSpec as P


AXES = ("rep", "shard")
DEPTH = 4
LEFT_ROWS = 256
FINAL_ROWS = 128
F32, BF16 = jnp.float32, jnp.bfloat16
HIGHEST = lax.Precision.HIGHEST
NT = (((1,), (1,)), ((), ()))
NN = (((1,), (0,)), ((), ()))
TT = (((0,), (1,)), ((), ()))
VMEM = pl.BlockSpec(memory_space=pltpu.VMEM)
SMEM = pl.BlockSpec(memory_space=pltpu.SMEM)
ANY = pl.BlockSpec(memory_space=pl.ANY)


def dot(a, b, dims, precision=None):
    return lax.dot_general(a, b, dims, precision=precision, preferred_element_type=F32)


def split(x):
    high = x.astype(BF16)
    return high, (x - high.astype(F32)).astype(BF16)


def params(mib):
    return pltpu.CompilerParams(vmem_limit_bytes=mib << 20)


def bit(code, index):
    return (code[0] >> index) & 1


def shape_of(*shape, dtype=F32):
    return jax.ShapeDtypeStruct(shape, dtype)


def left_kernel(block, jobs, code, grad, error, basis, *refs):
    outs, (grads, errors, factors, sems) = refs[-4 - 3 * len(jobs) : -4], refs[-4:]
    rank = basis.shape[1]
    copies = [pltpu.make_async_copy(basis, factors, sems.at[2, 0])]
    copies[0].start()
    blocks = []
    for job, (which, begin, end) in enumerate(jobs):
        w = bit(code, which)
        for start in range(begin, end, block):
            i = len(blocks)
            source, target = pl.ds(start, block), pl.ds(i * block, block)
            pair = (
                pltpu.make_async_copy(error.at[0, w, source], errors.at[target], sems.at[0, i]),
                pltpu.make_async_copy(grad.at[0, w, source], grads.at[target], sems.at[1, i]),
            )
            blocks.append((job, start, pair))

    def begin_block(i):
        if i < len(blocks):
            for copy in blocks[i][2]:
                copy.start()

    for i in range(DEPTH):
        begin_block(i)
    copies[0].wait()
    cuts = []
    for which, _, _ in jobs:
        top, rest = split(factors[bit(code, which)])
        cuts.append((top, jnp.concatenate([top, rest], axis=0)))
    for i, (job, start, pair) in enumerate(blocks):
        for copy in pair:
            copy.wait()
        begin_block(i + DEPTH)
        top, cut = cuts[job]
        high, low, left = outs[3 * job : 3 * job + 3]
        source, target = slice(start, start + block), slice(i * block, (i + 1) * block)
        upper, lower = split(grads[target].astype(F32) + errors[target])
        high[source] = upper
        low[source] = lower
        both = dot(cut, upper, NT)
        left[:, source] = both[:rank] + both[rank:] + dot(top, lower, NT)


def left_of(jobs, code, grad, error, basis, before=()):
    _, _, rows, cols = grad.shape
    rank = basis.shape[1]
    block = min(rows // 2, LEFT_ROWS)
    total = sum(end - begin for _, begin, end in jobs)
    return pl.pallas_call(
        functools.partial(left_kernel, block, jobs),
        name="left",
        in_specs=[SMEM, ANY, ANY, ANY] + [VMEM] * len(before),
        out_specs=[VMEM] * (3 * len(jobs)),
        out_shape=[
            shape_of(rows, cols, dtype=BF16),
            shape_of(rows, cols, dtype=BF16),
            shape_of(rank, rows),
        ]
        * len(jobs),
        scratch_shapes=[
            pltpu.VMEM((total, cols), BF16),
            pltpu.VMEM((total, cols), F32),
            pltpu.VMEM(basis.shape, F32),
            pltpu.SemaphoreType.DMA((3, total // block)),
        ],
        input_output_aliases={4 + k: k for k in range(len(before))},
        compiler_params=params(16),
        cost_estimate=pl.CostEstimate(
            flops=6 * total * cols * rank, bytes_accessed=10 * total * cols, transcendentals=0
        ),
    )(code, grad, error, basis, *before)


def ordered(left, keep):
    half = left.shape[0] // 2
    pick = lambda index: left[pl.ds(pl.multiple_of(index * half, half), half), :]
    return jnp.concatenate([pick(1 - keep), pick(keep)], axis=0)


def product(left, high, low, columns):
    rank = left.shape[0]
    top, rest = split(left)
    both = dot(jnp.concatenate([top, rest], axis=0), high[:, columns], NN)
    return both[:rank] + both[rank:] + dot(top, low[:, columns], NN)


def right_kernel(starts, keeps, with_gram, code, left, high, low, *outs):
    for start, keep, right in zip(starts, keeps, outs):
        columns = slice(start, start + right.shape[1])
        chosen = left[...] if keep is None else ordered(left, bit(code, keep))
        right[...] = product(chosen, high, low, columns)
    if with_gram:
        half = left.shape[0] // 2
        gram = dot(left[...], left[...], NT, HIGHEST)
        outs[-1][...] = jnp.concatenate([gram[:half], gram[half:]], axis=1)


def right_of(columns, keeps, code, left, high, low, with_gram=False):
    rows, _ = high.shape
    rank = left.shape[0]
    width = sum(width for _, width in columns)
    out_shape = [shape_of(rank, width) for _, width in columns]
    if with_gram:
        out_shape.append(shape_of(rank // 2, 2 * rank))
    return pl.pallas_call(
        functools.partial(right_kernel, [start for start, _ in columns], keeps, with_gram),
        name="right",
        in_specs=[SMEM] + [VMEM] * 3,
        out_specs=[VMEM] * len(out_shape),
        out_shape=out_shape,
        compiler_params=params(8),
        cost_estimate=pl.CostEstimate(
            flops=6 * rows * width * rank, bytes_accessed=4 * rows * width, transcendentals=0
        ),
    )(code, left, high, low)


def eliminate(whole, begin, end):
    rank = whole.shape[0]
    tile = 8
    work = [whole[i : i + tile] for i in range(0, rank, tile)]
    inside = lax.broadcasted_iota(jnp.int32, (tile, 1), 0)
    spread = lambda array: jnp.broadcast_to(array, (tile, 2 * rank))
    for j in range(begin, end, 2):
        home, at = divmod(j, tile)
        first, second = spread(work[home][at : at + 1]), spread(work[home][at + 1 : at + 2])
        a, b = spread(first[:, j : j + 1]), spread(first[:, j + 1 : j + 2])
        c = spread(second[:, j + 1 : j + 2])
        over = 1.0 / (a * c - b * b)
        one = (c * first - b * second) * over
        two = (a * second - b * first) * over
        for k in range(home, rank // tile):
            x, y = spread(work[k][:, j : j + 1]), spread(work[k][:, j + 1 : j + 2])
            if k == home:
                x = jnp.where(inside > at + 1, x, 0.0)
                y = jnp.where(inside > at + 1, y, 0.0)
            work[k] = work[k] - x * one - y * two
    return jnp.concatenate(work, axis=0)


def opening_kernel(end, packed, out):
    rank = out.shape[0]
    sums = packed[:, packed.shape[1] - 2 * rank :]
    row = lax.broadcasted_iota(jnp.int32, (rank, rank), 0)
    col = lax.broadcasted_iota(jnp.int32, (rank, rank), 1)
    gram = jnp.concatenate([sums[:, :rank], sums[:, rank:]], axis=0)
    whole = jnp.concatenate([gram, jnp.where(row == col, 1.0, 0.0)], axis=1)
    out[...] = eliminate(whole, 0, end)


def closing_kernel(begin, work, inverse):
    rank = inverse.shape[0]
    row = lax.broadcasted_iota(jnp.int32, (rank, 2 * rank), 0)
    col = lax.broadcasted_iota(jnp.int32, (rank, 2 * rank), 1)
    whole = eliminate(work[...], begin, rank - 2)
    above = jnp.concatenate([whole[-1:], whole[:-1]], axis=0)
    before = col == row - 1
    pick = lambda array, mask: jnp.sum(jnp.where(mask, array, 0.0), axis=1, keepdims=True)
    odd = row[:, :1] % 2 == 1
    pivot = jnp.where(odd, pick(above, before), 1.0)
    ratio = jnp.where(odd, pick(whole, before) / pivot, 0.0)
    whole = whole - ratio * above
    inverse[...] = whole[:, rank:] / jnp.sqrt(pick(whole, col == row))


def factor_of(kernel, array, rank, width):
    return pl.pallas_call(
        kernel,
        name="factor",
        in_specs=[VMEM],
        out_specs=VMEM,
        out_shape=shape_of(rank, width),
        compiler_params=params(8),
        cost_estimate=pl.CostEstimate(
            flops=2 * rank**3, bytes_accessed=8 * rank * rank, transcendentals=rank
        ),
    )(array)


def final_kernel(block, scale, keeps, code, *refs):
    update, new_error, basis_next, updates, errors, rights, sems = refs[-7:]
    count = (len(refs) - 7) // 2
    copies = []
    for which in range(2):
        inverse, left, high, low, *totals = refs[count * which : count * (which + 1)]
        rows = left.shape[1]
        w = bit(code, which)
        start = 0
        pieces = []
        for keep, total in zip(keeps, totals):
            columns = slice(start, start + total.shape[1])
            right = dot(inverse[...], ordered(total, 1 - bit(code, keep)) * scale, NN, HIGHEST)
            rights[which, :, columns] = right
            top, rest = split(right)
            pieces.append(jnp.concatenate([top, rest, top], axis=0))
            start += total.shape[1]
        pieces = jnp.concatenate(pieces, axis=1)
        copies.append(pltpu.make_async_copy(rights.at[which], basis_next.at[w], sems.at[which, 2, 0]))
        copies[-1].start()
        top, rest = split(dot(left[...], inverse[...], TT, HIGHEST))
        ortho = jnp.concatenate([top, top, rest], axis=1)
        for i, start in enumerate(range(0, rows, block)):
            part, where = slice(start, start + block), pl.ds(start, block)
            approx = dot(ortho[part], pieces, NN)
            updates[which, part] = approx.astype(BF16)
            errors[which, part] = (high[part].astype(F32) + low[part].astype(F32)) - approx
            for kind, source, target in (
                (0, errors.at[which, where], new_error.at[0, w, where]),
                (1, updates.at[which, where], update.at[w, where]),
            ):
                copies.append(pltpu.make_async_copy(source, target, sems.at[which, kind, i]))
                copies[-1].start()
    for copy in copies:
        copy.wait()


def final_of(keeps, code, mine, theirs, scale):
    rank, rows = mine[1].shape
    cols = mine[2].shape[1]
    block = min(rows, FINAL_ROWS)
    return pl.pallas_call(
        functools.partial(final_kernel, block, scale, keeps),
        name="final",
        in_specs=[SMEM] + [VMEM] * (2 * len(mine)),
        out_specs=[ANY] * 3,
        out_shape=[
            shape_of(2, rows, cols, dtype=BF16),
            shape_of(1, 2, rows, cols),
            shape_of(2, rank, cols),
        ],
        scratch_shapes=[
            pltpu.VMEM((2, rows, cols), BF16),
            pltpu.VMEM((2, rows, cols), F32),
            pltpu.VMEM((2, rank, cols), F32),
            pltpu.SemaphoreType.DMA((2, 3, rows // block)),
        ],
        compiler_params=params(24),
        cost_estimate=pl.CostEstimate(
            flops=12 * rows * cols * rank, bytes_accessed=20 * rows * cols, transcendentals=0
        ),
    )(code, *mine, *theirs)


def bits_of(count):
    return [1 << k for k in range(count.bit_length() - 1)]


def plan(replicas, shards):
    r = [(mask, 0) for mask in bits_of(replicas)[1:]]
    t = [(0, mask) for mask in bits_of(shards)]
    orders = (t + r, r + t)
    return r, t, orders


def on_device(replicas, shards, grad_kv, error_kv, basis_kv):
    def swap(value, masks):
        pairs = [
            (i * shards + j, (i ^ masks[0]) * shards + (j ^ masks[1]))
            for i in range(replicas)
            for j in range(shards)
        ]
        return lax.ppermute(value, AXES, pairs)

    def core(value):
        return swap(value, (1, 0))

    r, t, orders = plan(replicas, shards)
    scale = 1.0 / replicas

    rep, shard = lax.axis_index("rep"), lax.axis_index("shard")
    side = rep & 1
    code = side + 2 * (1 - side)
    for part, order in enumerate(orders):
        kept = ((rep & order[0][0]) + (shard & order[0][1]) > 0).astype(jnp.int32)
        code += kept << (2 + part)
    code = code.astype(jnp.int32).reshape(1)
    mine, theirs = 0, 1
    keeps = (2, 3)

    basis = basis_kv.transpose(0, 2, 1)
    grad_kv, error_kv, basis = (
        pltpu.with_memory_space_constraint(x, pltpu.HBM) for x in (grad_kv, error_kv, basis)
    )
    rank = basis.shape[1]
    rows, cols = grad_kv.shape[2:]

    ahead = rows // 2
    jobs = ((theirs, 0, rows), (mine, 0, ahead)), ((mine, ahead, rows),)
    high_t, low_t, left_t, *begun = left_of(jobs[0], code, grad_kv, error_kv, basis)
    arriving = core(left_t)
    high_m, low_m, left_m = left_of(jobs[1], code, grad_kv, error_kv, basis, begun)
    left_m = left_m + arriving
    for step in r:
        left_m = left_m + swap(left_m, step)
    left_m = left_m * scale
    left_t = core(left_m)

    first = cols * 3 // 8
    columns = ((0, first), (first, cols - first))
    *rights, gram = right_of(columns, keeps, code, left_m, high_m, low_m, True)
    arrivals = [
        core(right_of((columns[part],), (keeps[part],), code, left_t, high_t, low_t)[0])
        for part in range(2)
    ]
    totals_m, totals_t = [], []
    for part, (_, width) in enumerate(columns):
        right = rights[part] + arrivals[part]
        send, stay = right[: rank // 2], right[rank // 2 :]
        if part == 0:
            send, stay = (jnp.concatenate([x, gram], axis=1) for x in (send, stay))
        steps = orders[part]
        for turn, step in enumerate(steps):
            if part == 0 and turn == len(t):
                work = factor_of(functools.partial(opening_kernel, rank // 2), stay, rank, 2 * rank)
                inverse_m = factor_of(functools.partial(closing_kernel, rank // 2), work, rank, rank)
                stay = stay[:, :width]
            arrived = swap(send if turn == 0 else stay, step)
            stay = stay + arrived
        back = swap(stay, steps[0])
        total = jnp.concatenate([stay, back], axis=0)
        totals_m.append(total)
        totals_t.append(core(total))
    inverse_t = core(inverse_m)

    update, new_error, right = final_of(
        keeps,
        code,
        (inverse_m, left_m, high_m, low_m, *totals_m),
        (inverse_t, left_t, high_t, low_t, *totals_t),
        scale,
    )
    return update, new_error, right.transpose(0, 2, 1)


def solution(mesh):
    replicas, shards = mesh.shape["rep"], mesh.shape["shard"]
    placed = (P("rep", None, "shard", None), P("rep", None, "shard", None), P())

    def body(*args):
        return on_device(replicas, shards, *args)

    step = jax.shard_map(
        body,
        mesh=mesh,
        in_specs=placed,
        out_specs=(P(None, "shard", None), P("rep", None, "shard", None), P()),
        check_vma=False,
    )
    _, _, _ = plan(replicas, shards)
    return step
```

profile of v0, /device:TPU:0, one launch (start us, length us, event | category | flops | bytes accessed | tf_op | source)
XLA Modules:
  0.0 64.2 jit_solution(13487583839855363977)
XLA Ops:
  0.6 5.9 %left.2 = (bf16[1024,1024]{1,0:T(8,128)(2,1)S(1)}, bf16[1024,1024]{1,0:T(8,128)(2,1)S(1)}, f32[64,1024]{1,0:T(8,128)S(1)}, bf16[1024,1024]{1,0:T(8,128)(2,1)S(1)...) custom-call(s32[1]{0:T(128)} %bitcast.code, bf16[1,2,1024,1024]{3,2,1,0:T(8,128)(2,1)} %grad.3, ...), custom_call_target="tpu_custom_call" | custom-call | flops 603979776 | bytes 15728640 | tf_op jit(solution)/shard_map/left/pallas_call | solution.py:94
  6.6 0.6 collective-permute-start
  7.1 3.0 %left.3 = (bf16[1024,1024]{1,0:T(8,128)(2,1)S(1)}, bf16[1024,1024]{1,0:T(8,128)(2,1)S(1)}, f32[64,1024]{1,0:T(8,128)S(1)}) custom-call(s32[1]{0:T(128)} %bitcast.code, bf16[1,2,1024,1024]{3,2,1,0:T(8,128)(2,1)} %grad.3, f32[1,2,1024,1024]{3,2,1,0:T(8,128)} %error.3, ...), custom_call_target="tpu_custom_call", output_to_operand_aliasing={{0}: (4, {}), {1}: (5, {}), {2}: (6, {})} | custom-call | flops 201326592 | bytes 5242880 | tf_op jit(solution)/shard_map/left/pallas_call | solution.py:94
  10.1 0.0 collective-permute-done
  10.2 2.6 %collective-permute-start.1 = (f32[64,1024]{1,0:T(8,128)S(1)}, f32[64,1024]{1,0:T(8,128)S(1)}, u32[]{:S(2)}, u32[]{:S(2)}) collective-permute-start(f32[64,1024]{1,0:T(8,128)S(1)} %add.48), channel_id=1, source_target_pairs={{0,16},{1,17},{2,18},{3,19},{4,20},{5,21},{6,22},{7,23},{8,24},{9,... | collective-permute-start | bytes 786440 | tf_op jit(solution)/shard_map/ppermute | solution.py:307
  12.8 7.0 %collective-permute-done.1 = f32[64,1024]{1,0:T(8,128)S(1)} collective-permute-done((f32[64,1024]{1,0:T(8,128)S(1)}, f32[64,1024]{1,0:T(8,128)S(1)}, u32[]{:S(2)}, u32[]{:S(2)}) %collective-permute-start.1) | collective-permute-done | bytes 262176 | tf_op jit(solution)/shard_map/ppermute | solution.py:307
  19.8 0.1 collective-permute-start.2
  19.8 1.5 %collective-permute-done.2.left.refs_7_ = f32[64,1024]{1,0:T(8,128)S(1)} collective-permute-done((f32[64,1024]{1,0:T(8,128)S(1)}, f32[64,1024]{1,0:T(8,128)S(1)}, u32[]{:S(2)}, u32[]{:S(2)}) %collective-permute-start.2) | collective-permute-done | bytes 262176 | tf_op jit(solution)/shard_map/ppermute | solution.py:307
  21.4 0.4 right.4
  21.8 0.2 collective-permute-start.3
  22.0 1.1 %right.3 = (f32[64,384]{1,0:T(8,128)S(1)}, f32[64,640]{1,0:T(8,128)S(1)}, f32[32,128]{1,0:T(8,128)S(1)}) custom-call(s32[1]{0:T(128)} %bitcast.code, f32[64,1024]{1,0:T(8,128)S(1)} %add_multiply_fusion.left.refs_1_, bf16[1024,1024]{1,0:T(8,128)(2,1)S(1)} %get-tuple-element.23.high.refs_2_, bf16[1024,1024]{1,0:T(8,128)(2,1)S(1)} %get-tuple-element.24.low.refs_3_), custom_call_target="tpu_custom_call" | custom-call | flops 402653184 | bytes 4194304 | tf_op jit(solution)/shard_map/right/pallas_call | solution.py:150
  23.1 0.6 right.5
  23.7 0.4 collective-permute-start.9
  24.1 0.0 collective-permute-done.3
  24.2 1.0 %collective-permute-done.9 = f32[64,640]{1,0:T(8,128)S(1)} collective-permute-done((f32[64,640]{1,0:T(8,128)S(1)}, f32[64,640]{1,0:T(8,128)S(1)}, u32[]{:S(2)}, u32[]{:S(2)}) %collective-permute-start.9) | collective-permute-done | bytes 163872 | tf_op jit(solution)/shard_map/ppermute | solution.py:307
  25.2 1.8 %collective-permute-start.10 = (f32[32,640]{1,0:T(8,128)S(1)}, f32[32,640]{1,0:T(8,128)S(1)}, u32[]{:S(2)}, u32[]{:S(2)}) collective-permute-start(f32[32,640]{1,0:T(8,128)S(1)} %slice.24), channel_id=1, source_target_pairs={{0,16},{1,17},{2,18},{3,19},{4,20},{5,21},{6,22},{7,23},{8,24},{9,... | collective-permute-start | bytes 245768 | tf_op jit(solution)/shard_map/ppermute | solution.py:307
  27.0 1.5 %collective-permute-start.4 = (f32[32,512]{1,0:T(8,128)S(1)}, f32[32,512]{1,0:T(8,128)S(1)}, u32[]{:S(2)}, u32[]{:S(2)}) collective-permute-start(f32[32,512]{1,0:T(8,128)S(1)} %pad_maximum_fusion.2), channel_id=1, source_target_pairs={{0,1},{1,0},{2,3},{3,2},{4,5},{5,4},{6,7},{7,6},{8,9},{9,8},{10,11... | collective-permute-start | bytes 196616 | tf_op jit(solution)/shard_map/ppermute | solution.py:307
  28.5 1.5 %collective-permute-done.10 = f32[32,640]{1,0:T(8,128)S(1)} collective-permute-done((f32[32,640]{1,0:T(8,128)S(1)}, f32[32,640]{1,0:T(8,128)S(1)}, u32[]{:S(2)}, u32[]{:S(2)}) %collective-permute-start.10) | collective-permute-done | bytes 81952 | tf_op jit(solution)/shard_map/ppermute | solution.py:307
  30.0 1.8 %collective-permute-start.11 = (f32[32,640]{1,0:T(8,128)S(1)}, f32[32,640]{1,0:T(8,128)S(1)}, u32[]{:S(2)}, u32[]{:S(2)}) collective-permute-start(f32[32,640]{1,0:T(8,128)S(1)} %slice_add_fusion), channel_id=1, source_target_pairs={{0,1},{1,0},{2,3},{3,2},{4,5},{5,4},{6,7},{7,6},{8,9},{9,8},{10,11... | collective-permute-start | bytes 245768 | tf_op jit(solution)/shard_map/ppermute | solution.py:307
  31.8 0.0 collective-permute-done.4
  31.8 1.6 %collective-permute-start.5 = (f32[32,512]{1,0:T(8,128)S(1)}, f32[32,512]{1,0:T(8,128)S(1)}, u32[]{:S(2)}, u32[]{:S(2)}) collective-permute-start(f32[32,512]{1,0:T(8,128)S(1)} %fusion), channel_id=1, source_target_pairs={{0,2},{1,3},{2,0},{3,1},{4,6},{5,7},{6,4},{7,5},{8,10},{9,11},{10,... | collective-permute-start | bytes 196616 | tf_op jit(solution)/shard_map/ppermute | solution.py:307
  33.4 1.1 %collective-permute-done.11 = f32[32,640]{1,0:T(8,128)S(1)} collective-permute-done((f32[32,640]{1,0:T(8,128)S(1)}, f32[32,640]{1,0:T(8,128)S(1)}, u32[]{:S(2)}, u32[]{:S(2)}) %collective-permute-start.11) | collective-permute-done | bytes 81952 | tf_op jit(solution)/shard_map/ppermute | solution.py:307
  34.5 1.9 %collective-permute-start.12 = (f32[32,640]{1,0:T(8,128)S(1)}, f32[32,640]{1,0:T(8,128)S(1)}, u32[]{:S(2)}, u32[]{:S(2)}) collective-permute-start(f32[32,640]{1,0:T(8,128)S(1)} %add.57), channel_id=1, source_target_pairs={{0,2},{1,3},{2,0},{3,1},{4,6},{5,7},{6,4},{7,5},{8,10},{9,11},{10,... | collective-permute-start | bytes 245768 | tf_op jit(solution)/shard_map/ppermute | solution.py:307
  36.4 0.3 collective-permute-done.5
  36.7 2.5 %collective-permute-start.6 = (f32[32,512]{1,0:T(8,128)S(1)}, f32[32,512]{1,0:T(8,128)S(1)}, u32[]{:S(2)}, u32[]{:S(2)}) collective-permute-start(f32[32,512]{1,0:T(8,128)S(1)} %add.52), channel_id=1, source_target_pairs={{0,4},{1,5},{2,6},{3,7},{4,0},{5,1},{6,2},{7,3},{8,12},{9,13},{10,... | collective-permute-start | bytes 196616 | tf_op jit(solution)/shard_map/ppermute | solution.py:307
  39.2 0.5 collective-permute-done.12
  39.7 2.3 %collective-permute-start.13 = (f32[32,640]{1,0:T(8,128)S(1)}, f32[32,640]{1,0:T(8,128)S(1)}, u32[]{:S(2)}, u32[]{:S(2)}) collective-permute-start(f32[32,640]{1,0:T(8,128)S(1)} %add.58), channel_id=1, source_target_pairs={{0,4},{1,5},{2,6},{3,7},{4,0},{5,1},{6,2},{7,3},{8,12},{9,13},{10,... | collective-permute-start | bytes 245768 | tf_op jit(solution)/shard_map/ppermute | solution.py:307
  41.9 1.7 %collective-permute-done.6 = f32[32,512]{1,0:T(8,128)S(1)} collective-permute-done((f32[32,512]{1,0:T(8,128)S(1)}, f32[32,512]{1,0:T(8,128)S(1)}, u32[]{:S(2)}, u32[]{:S(2)}) %collective-permute-start.6) | collective-permute-done | bytes 65568 | tf_op jit(solution)/shard_map/ppermute | solution.py:307
  43.7 1.6 %collective-permute-start.7 = (f32[32,384]{1,0:T(8,128)S(1)}, f32[32,384]{1,0:T(8,128)S(1)}, u32[]{:S(2)}, u32[]{:S(2)}) collective-permute-start(f32[32,384]{1,0:T(8,128)S(1)} %slice.22), channel_id=1, source_target_pairs={{0,16},{1,17},{2,18},{3,19},{4,20},{5,21},{6,22},{7,23},{8,24},{9,... | collective-permute-start | bytes 147464 | tf_op jit(solution)/shard_map/ppermute | solution.py:307
  45.2 0.0 collective-permute-done.13
  45.3 1.4 %collective-permute-start.14 = (f32[32,640]{1,0:T(8,128)S(1)}, f32[32,640]{1,0:T(8,128)S(1)}, u32[]{:S(2)}, u32[]{:S(2)}) collective-permute-start(f32[32,640]{1,0:T(8,128)S(1)} %add.59), channel_id=1, source_target_pairs={{0,16},{1,17},{2,18},{3,19},{4,20},{5,21},{6,22},{7,23},{8,24},{9,... | collective-permute-start | bytes 245768 | tf_op jit(solution)/shard_map/ppermute | solution.py:307
  46.7 1.1 %collective-permute-done.7 = f32[32,384]{1,0:T(8,128)S(1)} collective-permute-done((f32[32,384]{1,0:T(8,128)S(1)}, f32[32,384]{1,0:T(8,128)S(1)}, u32[]{:S(2)}, u32[]{:S(2)}) %collective-permute-start.7) | collective-permute-done | bytes 49184 | tf_op jit(solution)/shard_map/ppermute | solution.py:307
  47.8 1.5 %collective-permute-start.8 = (f32[32,384]{1,0:T(8,128)S(1)}, f32[32,384]{1,0:T(8,128)S(1)}, u32[]{:S(2)}, u32[]{:S(2)}) collective-permute-start(f32[32,384]{1,0:T(8,128)S(1)} %slice_add_fusion.1), channel_id=1, source_target_pairs={{0,1},{1,0},{2,3},{3,2},{4,5},{5,4},{6,7},{7,6},{8,9},{9,8},{10,11... | collective-permute-start | bytes 147464 | tf_op jit(solution)/shard_map/ppermute | solution.py:307
  49.3 0.4 collective-permute-done.14
  49.8 0.1 collective-permute-start.17
  49.9 2.1 %collective-permute-done.8 = f32[32,384]{1,0:T(8,128)S(1)} collective-permute-done((f32[32,384]{1,0:T(8,128)S(1)}, f32[32,384]{1,0:T(8,128)S(1)}, u32[]{:S(2)}, u32[]{:S(2)}) %collective-permute-start.8) | collective-permute-done | bytes 49184 | tf_op jit(solution)/shard_map/ppermute | solution.py:307
  52.0 0.1 collective-permute-start.16
  52.1 2.3 %factor.2.work = f32[64,128]{1,0:T(8,128)S(1)} custom-call(f32[32,512]{1,0:T(8,128)S(1)} %add.53.packed), custom_call_target="tpu_custom_call" | custom-call | flops 524288 | bytes 32768 | tf_op jit(solution)/shard_map/factor/pallas_call | solution.py:212
  54.3 2.1 %factor.3.refs_0_ = f32[64,64]{1,0:T(8,128)S(1)} custom-call(f32[64,128]{1,0:T(8,128)S(1)} %factor.2.work), custom_call_target="tpu_custom_call" | custom-call | flops 524288 | bytes 32768 | tf_op jit(solution)/shard_map/factor/pallas_call | solution.py:212
  56.4 0.5 collective-permute-start.15
  56.9 0.9 %collective-permute-done.15.refs_6_ = f32[64,64]{1,0:T(8,128)S(1)} collective-permute-done((f32[64,64]{1,0:T(8,128)S(1)}, f32[64,64]{1,0:T(8,128)S(1)}, u32[]{:S(2)}, u32[]{:S(2)}) %collective-permute-start.15) | collective-permute-done | bytes 16416 | tf_op jit(solution)/shard_map/ppermute | solution.py:307
  57.8 0.0 collective-permute-done.16.refs_10_
  57.8 0.0 collective-permute-done.17.refs_11_
  57.8 6.4 %final.1 = (bf16[2,1024,1024]{2,1,0:T(8,128)(2,1)}, f32[1,2,1024,1024]{3,2,1,0:T(8,128)}, f32[2,64,1024]{2,1,0:T(8,128)}) custom-call(s32[1]{0:T(128)} %bitcast.code, f32[64,64]{1,0:T(8,128)S(1)} %factor.3.refs_0_, f32[64,1024]{1,0:T(8,128)S(1)} %add_multiply_fusion.left.refs_1_, bf16[1024,1024]{1,0:T(8,128)(2,1)S(1)} %get-tuple-element.23.high.refs_2_, ...), custom_call_target="tpu_custom_call" | custom-call | flops 805306368 | bytes 20971520 | tf_op jit(solution)/shard_map/final/pallas_call | solution.py:266
  (18 shorter events, 0.2 us)
Async XLA Ops:
  6.6 3.5 %collective-permute-start = (f32[64,1024]{1,0:T(8,128)S(1)}, f32[64,1024]{1,0:T(8,128)S(1)}, u32[]{:S(2)}, u32[]{:S(2)}) collective-permute-start(f32[64,1024]{1,0:T(8,128)S(1)} %get-tuple-element.22), channel_id=1, source_target_pairs={{0,8},{1,9},{2,10},{3,11},{4,12},{5,13},{6,14},{7,15},{8,0},{9,1},... | collective-permute-start | bytes 786440 | tf_op jit(solution)/shard_map/ppermute | solution.py:307
  10.2 9.6 %collective-permute-start.1 = (f32[64,1024]{1,0:T(8,128)S(1)}, f32[64,1024]{1,0:T(8,128)S(1)}, u32[]{:S(2)}, u32[]{:S(2)}) collective-permute-start(f32[64,1024]{1,0:T(8,128)S(1)} %add.48), channel_id=1, source_target_pairs={{0,16},{1,17},{2,18},{3,19},{4,20},{5,21},{6,22},{7,23},{8,24},{9,... | collective-permute-start | bytes 786440 | tf_op jit(solution)/shard_map/ppermute | solution.py:307
  19.8 1.6 %collective-permute-start.2 = (f32[64,1024]{1,0:T(8,128)S(1)}, f32[64,1024]{1,0:T(8,128)S(1)}, u32[]{:S(2)}, u32[]{:S(2)}) collective-permute-start(f32[64,1024]{1,0:T(8,128)S(1)} %add_multiply_fusion.left.refs_1_), channel_id=1, source_target_pairs={{0,8},{1,9},{2,10},{3,11},{4,12},{5,13},{6,14},{7,15},{8,0},{9,1},... | collective-permute-start | bytes 786440 | tf_op jit(solution)/shard_map/ppermute | solution.py:307
  21.8 2.4 %collective-permute-start.3 = (f32[64,384]{1,0:T(8,128)S(1)}, f32[64,384]{1,0:T(8,128)S(1)}, u32[]{:S(2)}, u32[]{:S(2)}) collective-permute-start(f32[64,384]{1,0:T(8,128)S(1)} %right.4), channel_id=1, source_target_pairs={{0,8},{1,9},{2,10},{3,11},{4,12},{5,13},{6,14},{7,15},{8,0},{9,1},... | collective-permute-start | bytes 294920 | tf_op jit(solution)/shard_map/ppermute | solution.py:307
  23.7 1.5 %collective-permute-start.9 = (f32[64,640]{1,0:T(8,128)S(1)}, f32[64,640]{1,0:T(8,128)S(1)}, u32[]{:S(2)}, u32[]{:S(2)}) collective-permute-start(f32[64,640]{1,0:T(8,128)S(1)} %right.5), channel_id=1, source_target_pairs={{0,8},{1,9},{2,10},{3,11},{4,12},{5,13},{6,14},{7,15},{8,0},{9,1},... | collective-permute-start | bytes 491528 | tf_op jit(solution)/shard_map/ppermute | solution.py:307
  25.2 4.8 %collective-permute-start.10 = (f32[32,640]{1,0:T(8,128)S(1)}, f32[32,640]{1,0:T(8,128)S(1)}, u32[]{:S(2)}, u32[]{:S(2)}) collective-permute-start(f32[32,640]{1,0:T(8,128)S(1)} %slice.24), channel_id=1, source_target_pairs={{0,16},{1,17},{2,18},{3,19},{4,20},{5,21},{6,22},{7,23},{8,24},{9,... | collective-permute-start | bytes 245768 | tf_op jit(solution)/shard_map/ppermute | solution.py:307
  27.0 4.8 %collective-permute-start.4 = (f32[32,512]{1,0:T(8,128)S(1)}, f32[32,512]{1,0:T(8,128)S(1)}, u32[]{:S(2)}, u32[]{:S(2)}) collective-permute-start(f32[32,512]{1,0:T(8,128)S(1)} %pad_maximum_fusion.2), channel_id=1, source_target_pairs={{0,1},{1,0},{2,3},{3,2},{4,5},{5,4},{6,7},{7,6},{8,9},{9,8},{10,11... | collective-permute-start | bytes 196616 | tf_op jit(solution)/shard_map/ppermute | solution.py:307
  30.0 4.5 %collective-permute-start.11 = (f32[32,640]{1,0:T(8,128)S(1)}, f32[32,640]{1,0:T(8,128)S(1)}, u32[]{:S(2)}, u32[]{:S(2)}) collective-permute-start(f32[32,640]{1,0:T(8,128)S(1)} %slice_add_fusion), channel_id=1, source_target_pairs={{0,1},{1,0},{2,3},{3,2},{4,5},{5,4},{6,7},{7,6},{8,9},{9,8},{10,11... | collective-permute-start | bytes 245768 | tf_op jit(solution)/shard_map/ppermute | solution.py:307
  31.8 4.9 %collective-permute-start.5 = (f32[32,512]{1,0:T(8,128)S(1)}, f32[32,512]{1,0:T(8,128)S(1)}, u32[]{:S(2)}, u32[]{:S(2)}) collective-permute-start(f32[32,512]{1,0:T(8,128)S(1)} %fusion), channel_id=1, source_target_pairs={{0,2},{1,3},{2,0},{3,1},{4,6},{5,7},{6,4},{7,5},{8,10},{9,11},{10,... | collective-permute-start | bytes 196616 | tf_op jit(solution)/shard_map/ppermute | solution.py:307
  34.5 5.1 %collective-permute-start.12 = (f32[32,640]{1,0:T(8,128)S(1)}, f32[32,640]{1,0:T(8,128)S(1)}, u32[]{:S(2)}, u32[]{:S(2)}) collective-permute-start(f32[32,640]{1,0:T(8,128)S(1)} %add.57), channel_id=1, source_target_pairs={{0,2},{1,3},{2,0},{3,1},{4,6},{5,7},{6,4},{7,5},{8,10},{9,11},{10,... | collective-permute-start | bytes 245768 | tf_op jit(solution)/shard_map/ppermute | solution.py:307
  36.7 7.0 %collective-permute-start.6 = (f32[32,512]{1,0:T(8,128)S(1)}, f32[32,512]{1,0:T(8,128)S(1)}, u32[]{:S(2)}, u32[]{:S(2)}) collective-permute-start(f32[32,512]{1,0:T(8,128)S(1)} %add.52), channel_id=1, source_target_pairs={{0,4},{1,5},{2,6},{3,7},{4,0},{5,1},{6,2},{7,3},{8,12},{9,13},{10,... | collective-permute-start | bytes 196616 | tf_op jit(solution)/shard_map/ppermute | solution.py:307
  39.7 5.6 %collective-permute-start.13 = (f32[32,640]{1,0:T(8,128)S(1)}, f32[32,640]{1,0:T(8,128)S(1)}, u32[]{:S(2)}, u32[]{:S(2)}) collective-permute-start(f32[32,640]{1,0:T(8,128)S(1)} %add.58), channel_id=1, source_target_pairs={{0,4},{1,5},{2,6},{3,7},{4,0},{5,1},{6,2},{7,3},{8,12},{9,13},{10,... | collective-permute-start | bytes 245768 | tf_op jit(solution)/shard_map/ppermute | solution.py:307
  43.7 4.2 %collective-permute-start.7 = (f32[32,384]{1,0:T(8,128)S(1)}, f32[32,384]{1,0:T(8,128)S(1)}, u32[]{:S(2)}, u32[]{:S(2)}) collective-permute-start(f32[32,384]{1,0:T(8,128)S(1)} %slice.22), channel_id=1, source_target_pairs={{0,16},{1,17},{2,18},{3,19},{4,20},{5,21},{6,22},{7,23},{8,24},{9,... | collective-permute-start | bytes 147464 | tf_op jit(solution)/shard_map/ppermute | solution.py:307
  45.3 4.5 %collective-permute-start.14 = (f32[32,640]{1,0:T(8,128)S(1)}, f32[32,640]{1,0:T(8,128)S(1)}, u32[]{:S(2)}, u32[]{:S(2)}) collective-permute-start(f32[32,640]{1,0:T(8,128)S(1)} %add.59), channel_id=1, source_target_pairs={{0,16},{1,17},{2,18},{3,19},{4,20},{5,21},{6,22},{7,23},{8,24},{9,... | collective-permute-start | bytes 245768 | tf_op jit(solution)/shard_map/ppermute | solution.py:307
  47.8 4.2 %collective-permute-start.8 = (f32[32,384]{1,0:T(8,128)S(1)}, f32[32,384]{1,0:T(8,128)S(1)}, u32[]{:S(2)}, u32[]{:S(2)}) collective-permute-start(f32[32,384]{1,0:T(8,128)S(1)} %slice_add_fusion.1), channel_id=1, source_target_pairs={{0,1},{1,0},{2,3},{3,2},{4,5},{5,4},{6,7},{7,6},{8,9},{9,8},{10,11... | collective-permute-start | bytes 147464 | tf_op jit(solution)/shard_map/ppermute | solution.py:307
  49.8 8.0 %collective-permute-start.17 = (f32[64,640]{1,0:T(8,128)S(1)}, f32[64,640]{1,0:T(8,128)S(1)}, u32[]{:S(2)}, u32[]{:S(2)}) collective-permute-start(f32[64,640]{1,0:T(8,128)S(1)} %pad_maximum_fusion.refs_5_), channel_id=1, source_target_pairs={{0,8},{1,9},{2,10},{3,11},{4,12},{5,13},{6,14},{7,15},{8,0},{9,1},... | collective-permute-start | bytes 491528 | tf_op jit(solution)/shard_map/ppermute | solution.py:307
  52.0 5.8 %collective-permute-start.16 = (f32[64,384]{1,0:T(8,128)S(1)}, f32[64,384]{1,0:T(8,128)S(1)}, u32[]{:S(2)}, u32[]{:S(2)}) collective-permute-start(f32[64,384]{1,0:T(8,128)S(1)} %pad_maximum_fusion.1.refs_4_), channel_id=1, source_target_pairs={{0,8},{1,9},{2,10},{3,11},{4,12},{5,13},{6,14},{7,15},{8,0},{9,1},... | collective-permute-start | bytes 294920 | tf_op jit(solution)/shard_map/ppermute | solution.py:307
  56.4 1.4 %collective-permute-start.15 = (f32[64,64]{1,0:T(8,128)S(1)}, f32[64,64]{1,0:T(8,128)S(1)}, u32[]{:S(2)}, u32[]{:S(2)}) collective-permute-start(f32[64,64]{1,0:T(8,128)S(1)} %factor.3.refs_0_), channel_id=1, source_target_pairs={{0,8},{1,9},{2,10},{3,11},{4,12},{5,13},{6,14},{7,15},{8,0},{9,1},... | collective-permute-start | bytes 49160 | tf_op jit(solution)/shard_map/ppermute | solution.py:307
where the time goes:
time: 64.3 us; the launch traced here: 64.2 us
  starting transfers between devices  22.3 us (35%)
  Pallas kernels  21.8 us (34%)
  waiting for transfers between devices  19 us (30%)
  between operations  0.8 us (1%)
    ppermute x18, starting transfers between devices, swap(): return lax.ppermute(value, AXES, pairs)  22.3 us
    ppermute x18, waiting for transfers between devices, swap(): return lax.ppermute(value, AXES, pairs)  19 us
    pallas_call x2, Pallas kernels, left_of(): pl.pallas_call(functools.partial(left_kernel, block, jobs), name='left',...  8.91 us
    pallas_call x1, Pallas kernels, final_of(): pl.pallas_call(functools.partial(final_kernel, block, scale, keeps), name...  6.39 us
    pallas_call x2, Pallas kernels, factor_of(): pl.pallas_call(kernel, name='factor', in_specs=[VMEM], out_specs=VMEM, ou...  4.35 us
    pallas_call x3, Pallas kernels, right_of(): pl.pallas_call(functools.partial(right_kernel, [start for start, _ in col...  2.14 us
  transfers between devices with their start and end apart: 18, of which 12 were waited for; matrix products, arithmetic and copies ran while one was open for 0% of the time, Pallas kernels for 14%

commit v1 on v0

--- a/solution.py
+++ b/solution.py
@@ -10,7 +10,7 @@
 
 AXES = ("rep", "shard")
 DEPTH = 4
-LEFT_ROWS = 256
+LEFT_ROWS = 512
 FINAL_ROWS = 128
 F32, BF16 = jnp.float32, jnp.bfloat16
 HIGHEST = lax.Precision.HIGHEST
@@ -44,7 +44,7 @@
 
 
 def left_kernel(block, jobs, code, grad, error, basis, *refs):
-    outs, (grads, errors, factors, sems) = refs[-4 - 3 * len(jobs) : -4], refs[-4:]
+    outs, (grads, errors, factors, sems) = refs[:-4], refs[-4:]
     rank = basis.shape[1]
     copies = [pltpu.make_async_copy(basis, factors, sems.at[2, 0])]
     copies[0].start()
@@ -86,15 +86,15 @@
         left[:, source] = both[:rank] + both[rank:] + dot(top, lower, NT)
 
 
-def left_of(jobs, code, grad, error, basis, before=()):
+def left_of(jobs, code, grad, error, basis):
     _, _, rows, cols = grad.shape
     rank = basis.shape[1]
-    block = min(rows // 2, LEFT_ROWS)
+    block = min(rows, LEFT_ROWS)
     total = sum(end - begin for _, begin, end in jobs)
     return pl.pallas_call(
         functools.partial(left_kernel, block, jobs),
         name="left",
-        in_specs=[SMEM, ANY, ANY, ANY] + [VMEM] * len(before),
+        in_specs=[SMEM, ANY, ANY, ANY],
         out_specs=[VMEM] * (3 * len(jobs)),
         out_shape=[
             shape_of(rows, cols, dtype=BF16),
@@ -108,12 +108,11 @@
             pltpu.VMEM(basis.shape, F32),
             pltpu.SemaphoreType.DMA((3, total // block)),
         ],
-        input_output_aliases={4 + k: k for k in range(len(before))},
-        compiler_params=params(16),
+        compiler_params=params(24),
         cost_estimate=pl.CostEstimate(
             flops=6 * total * cols * rank, bytes_accessed=10 * total * cols, transcendentals=0
         ),
-    )(code, grad, error, basis, *before)
+    )(code, grad, error, basis)
 
 
 def ordered(left, keep):
@@ -329,11 +328,9 @@
     rank = basis.shape[1]
     rows, cols = grad_kv.shape[2:]
 
-    ahead = rows // 2
-    jobs = ((theirs, 0, rows), (mine, 0, ahead)), ((mine, ahead, rows),)
-    high_t, low_t, left_t, *begun = left_of(jobs[0], code, grad_kv, error_kv, basis)
+    jobs = (theirs, 0, rows), (mine, 0, rows)
+    high_t, low_t, left_t, high_m, low_m, left_m = left_of(jobs, code, grad_kv, error_kv, basis)
     arriving = core(left_t)
-    high_m, low_m, left_m = left_of(jobs[1], code, grad_kv, error_kv, basis, begun)
     left_m = left_m + arriving
     for step in r:
         left_m = left_m + swap(left_m, step)

time: 64.3 us -> 62.4 us (0.970)
  Pallas kernels: 21.8 us -> 18.7 us
  waiting for transfers between devices: 19 us -> 19.9 us
    pallas_call x2 -> x1, Pallas kernels: 8.91 us -> 5.8 us  [left_of(): pl.pallas_call(functools.partial(left_kernel, block, jobs), name='left',...]
    ppermute x18, waiting for transfers between devices: 19 us -> 19.9 us  [swap(): return lax.ppermute(value, AXES, pairs)]
  transfers between devices with their start and end apart: 18 -> 18, of which waited for: 12 -> 13; matrix products, arithmetic and copies ran while one was open for 0% -> 0% of each run, Pallas kernels for 14% -> 10%
where the time goes in v1:
time: 62.4 us; the launch traced here: 62.2 us
  starting transfers between devices  22.7 us (36%)
  waiting for transfers between devices  19.9 us (32%)
  Pallas kernels  18.7 us (30%)
  between operations  0.78 us (1%)
    ppermute x18, starting transfers between devices, swap(): return lax.ppermute(value, AXES, pairs)  22.7 us
    ppermute x18, waiting for transfers between devices, swap(): return lax.ppermute(value, AXES, pairs)  19.9 us
    pallas_call x1, Pallas kernels, final_of(): pl.pallas_call(functools.partial(final_kernel, block, scale, keeps), name...  6.39 us
    pallas_call x1, Pallas kernels, left_of(): pl.pallas_call(functools.partial(left_kernel, block, jobs), name='left',...  5.8 us
    pallas_call x2, Pallas kernels, factor_of(): pl.pallas_call(kernel, name='factor', in_specs=[VMEM], out_specs=VMEM, ou...  4.35 us
    pallas_call x3, Pallas kernels, right_of(): pl.pallas_call(functools.partial(right_kernel, [start for start, _ in col...  2.13 us
  transfers between devices with their start and end apart: 18, of which 13 were waited for; matrix products, arithmetic and copies ran while one was open for 0% of the time, Pallas kernels for 10%

profile of v1, /device:TPU:0, one launch (start us, length us, event | category | flops | bytes accessed | tf_op | source)
XLA Modules:
  0.0 62.2 jit_solution(11972460471615489656)
XLA Ops:
  0.6 5.8 %left.1 = (bf16[1024,1024]{1,0:T(8,128)(2,1)S(1)}, bf16[1024,1024]{1,0:T(8,128)(2,1)S(1)}, f32[64,1024]{1,0:T(8,128)S(1)}, bf16[1024,1024]{1,0:T(8,128)(2,1)S(1)...) custom-call(s32[1]{0:T(128)} %bitcast.code, bf16[1,2,1024,1024]{3,2,1,0:T(8,128)(2,1)} %grad.1, ...), custom_call_target="tpu_custom_call" | custom-call | flops 805306368 | bytes 20971520 | tf_op jit(solution)/shard_map/left/pallas_call | solution.py:94
  6.4 0.6 collective-permute-start
  7.0 1.2 %collective-permute-done = f32[64,1024]{1,0:T(8,128)S(1)} collective-permute-done((f32[64,1024]{1,0:T(8,128)S(1)}, f32[64,1024]{1,0:T(8,128)S(1)}, u32[]{:S(2)}, u32[]{:S(2)}) %collective-permute-start) | collective-permute-done | bytes 262176 | tf_op jit(solution)/shard_map/ppermute | solution.py:306
  8.2 3.0 %collective-permute-start.1 = (f32[64,1024]{1,0:T(8,128)S(1)}, f32[64,1024]{1,0:T(8,128)S(1)}, u32[]{:S(2)}, u32[]{:S(2)}) collective-permute-start(f32[64,1024]{1,0:T(8,128)S(1)} %add.48), channel_id=1, source_target_pairs={{0,16},{1,17},{2,18},{3,19},{4,20},{5,21},{6,22},{7,23},{8,24},{9,... | collective-permute-start | bytes 786440 | tf_op jit(solution)/shard_map/ppermute | solution.py:306
  11.1 6.6 %collective-permute-done.1 = f32[64,1024]{1,0:T(8,128)S(1)} collective-permute-done((f32[64,1024]{1,0:T(8,128)S(1)}, f32[64,1024]{1,0:T(8,128)S(1)}, u32[]{:S(2)}, u32[]{:S(2)}) %collective-permute-start.1) | collective-permute-done | bytes 262176 | tf_op jit(solution)/shard_map/ppermute | solution.py:306
  17.8 0.1 collective-permute-start.2
  17.9 1.5 %collective-permute-done.2.left.refs_7_ = f32[64,1024]{1,0:T(8,128)S(1)} collective-permute-done((f32[64,1024]{1,0:T(8,128)S(1)}, f32[64,1024]{1,0:T(8,128)S(1)}, u32[]{:S(2)}, u32[]{:S(2)}) %collective-permute-start.2) | collective-permute-done | bytes 262176 | tf_op jit(solution)/shard_map/ppermute | solution.py:306
  19.4 0.4 right.4
  19.8 0.2 collective-permute-start.3
  20.0 1.1 %right.3 = (f32[64,384]{1,0:T(8,128)S(1)}, f32[64,640]{1,0:T(8,128)S(1)}, f32[32,128]{1,0:T(8,128)S(1)}) custom-call(s32[1]{0:T(128)} %bitcast.code, f32[64,1024]{1,0:T(8,128)S(1)} %add_multiply_fusion.left.refs_1_, bf16[1024,1024]{1,0:T(8,128)(2,1)S(1)} %get-tuple-element.17.high.refs_2_, bf16[1024,1024]{1,0:T(8,128)(2,1)S(1)} %get-tuple-element.18.low.refs_3_), custom_call_target="tpu_custom_call" | custom-call | flops 402653184 | bytes 4194304 | tf_op jit(solution)/shard_map/right/pallas_call | solution.py:149
  21.1 0.6 %right.5 = f32[64,640]{1,0:T(8,128)S(1)} custom-call(s32[1]{0:T(128)} %bitcast.code, f32[64,1024]{1,0:T(8,128)S(1)} %collective-permute-done.2.left.refs_7_, bf16[1024,1024]{1,0:T(8,128)(2,1)S(1)} %get-tuple-element.20.high.refs_8_, bf16[1024,1024]{1,0:T(8,128)(2,1)S(1)} %get-tuple-element.21.low.refs_9_), custom_call_target="tpu_custom_call" | custom-call | flops 251658240 | bytes 2621440 | tf_op jit(solution)/shard_map/right/pallas_call | solution.py:149
  21.7 0.4 collective-permute-start.9
  22.2 0.0 collective-permute-done.3
  22.2 1.0 %collective-permute-done.9 = f32[64,640]{1,0:T(8,128)S(1)} collective-permute-done((f32[64,640]{1,0:T(8,128)S(1)}, f32[64,640]{1,0:T(8,128)S(1)}, u32[]{:S(2)}, u32[]{:S(2)}) %collective-permute-start.9) | collective-permute-done | bytes 163872 | tf_op jit(solution)/shard_map/ppermute | solution.py:306
  23.2 1.8 %collective-permute-start.10 = (f32[32,640]{1,0:T(8,128)S(1)}, f32[32,640]{1,0:T(8,128)S(1)}, u32[]{:S(2)}, u32[]{:S(2)}) collective-permute-start(f32[32,640]{1,0:T(8,128)S(1)} %slice.24), channel_id=1, source_target_pairs={{0,16},{1,17},{2,18},{3,19},{4,20},{5,21},{6,22},{7,23},{8,24},{9,... | collective-permute-start | bytes 245768 | tf_op jit(solution)/shard_map/ppermute | solution.py:306
  25.1 1.5 %collective-permute-start.4 = (f32[32,512]{1,0:T(8,128)S(1)}, f32[32,512]{1,0:T(8,128)S(1)}, u32[]{:S(2)}, u32[]{:S(2)}) collective-permute-start(f32[32,512]{1,0:T(8,128)S(1)} %pad_maximum_fusion.2), channel_id=1, source_target_pairs={{0,1},{1,0},{2,3},{3,2},{4,5},{5,4},{6,7},{7,6},{8,9},{9,8},{10,11... | collective-permute-start | bytes 196616 | tf_op jit(solution)/shard_map/ppermute | solution.py:306
  26.5 1.5 %collective-permute-done.10 = f32[32,640]{1,0:T(8,128)S(1)} collective-permute-done((f32[32,640]{1,0:T(8,128)S(1)}, f32[32,640]{1,0:T(8,128)S(1)}, u32[]{:S(2)}, u32[]{:S(2)}) %collective-permute-start.10) | collective-permute-done | bytes 81952 | tf_op jit(solution)/shard_map/ppermute | solution.py:306
  28.0 1.8 %collective-permute-start.11 = (f32[32,640]{1,0:T(8,128)S(1)}, f32[32,640]{1,0:T(8,128)S(1)}, u32[]{:S(2)}, u32[]{:S(2)}) collective-permute-start(f32[32,640]{1,0:T(8,128)S(1)} %slice_add_fusion), channel_id=1, source_target_pairs={{0,1},{1,0},{2,3},{3,2},{4,5},{5,4},{6,7},{7,6},{8,9},{9,8},{10,11... | collective-permute-start | bytes 245768 | tf_op jit(solution)/shard_map/ppermute | solution.py:306
  29.8 0.0 collective-permute-done.4
  29.8 1.6 %collective-permute-start.5 = (f32[32,512]{1,0:T(8,128)S(1)}, f32[32,512]{1,0:T(8,128)S(1)}, u32[]{:S(2)}, u32[]{:S(2)}) collective-permute-start(f32[32,512]{1,0:T(8,128)S(1)} %fusion), channel_id=1, source_target_pairs={{0,2},{1,3},{2,0},{3,1},{4,6},{5,7},{6,4},{7,5},{8,10},{9,11},{10,... | collective-permute-start | bytes 196616 | tf_op jit(solution)/shard_map/ppermute | solution.py:306
  31.5 1.1 %collective-permute-done.11 = f32[32,640]{1,0:T(8,128)S(1)} collective-permute-done((f32[32,640]{1,0:T(8,128)S(1)}, f32[32,640]{1,0:T(8,128)S(1)}, u32[]{:S(2)}, u32[]{:S(2)}) %collective-permute-start.11) | collective-permute-done | bytes 81952 | tf_op jit(solution)/shard_map/ppermute | solution.py:306
  32.6 1.9 %collective-permute-start.12 = (f32[32,640]{1,0:T(8,128)S(1)}, f32[32,640]{1,0:T(8,128)S(1)}, u32[]{:S(2)}, u32[]{:S(2)}) collective-permute-start(f32[32,640]{1,0:T(8,128)S(1)} %add.57), channel_id=1, source_target_pairs={{0,2},{1,3},{2,0},{3,1},{4,6},{5,7},{6,4},{7,5},{8,10},{9,11},{10,... | collective-permute-start | bytes 245768 | tf_op jit(solution)/shard_map/ppermute | solution.py:306
  34.4 0.3 collective-permute-done.5
  34.7 2.5 %collective-permute-start.6 = (f32[32,512]{1,0:T(8,128)S(1)}, f32[32,512]{1,0:T(8,128)S(1)}, u32[]{:S(2)}, u32[]{:S(2)}) collective-permute-start(f32[32,512]{1,0:T(8,128)S(1)} %add.52), channel_id=1, source_target_pairs={{0,4},{1,5},{2,6},{3,7},{4,0},{5,1},{6,2},{7,3},{8,12},{9,13},{10,... | collective-permute-start | bytes 196616 | tf_op jit(solution)/shard_map/ppermute | solution.py:306
  37.2 0.5 collective-permute-done.12
  37.7 2.2 %collective-permute-start.13 = (f32[32,640]{1,0:T(8,128)S(1)}, f32[32,640]{1,0:T(8,128)S(1)}, u32[]{:S(2)}, u32[]{:S(2)}) collective-permute-start(f32[32,640]{1,0:T(8,128)S(1)} %add.58), channel_id=1, source_target_pairs={{0,4},{1,5},{2,6},{3,7},{4,0},{5,1},{6,2},{7,3},{8,12},{9,13},{10,... | collective-permute-start | bytes 245768 | tf_op jit(solution)/shard_map/ppermute | solution.py:306
  39.9 1.7 %collective-permute-done.6 = f32[32,512]{1,0:T(8,128)S(1)} collective-permute-done((f32[32,512]{1,0:T(8,128)S(1)}, f32[32,512]{1,0:T(8,128)S(1)}, u32[]{:S(2)}, u32[]{:S(2)}) %collective-permute-start.6) | collective-permute-done | bytes 65568 | tf_op jit(solution)/shard_map/ppermute | solution.py:306
  41.7 1.6 %collective-permute-start.7 = (f32[32,384]{1,0:T(8,128)S(1)}, f32[32,384]{1,0:T(8,128)S(1)}, u32[]{:S(2)}, u32[]{:S(2)}) collective-permute-start(f32[32,384]{1,0:T(8,128)S(1)} %slice.22), channel_id=1, source_target_pairs={{0,16},{1,17},{2,18},{3,19},{4,20},{5,21},{6,22},{7,23},{8,24},{9,... | collective-permute-start | bytes 147464 | tf_op jit(solution)/shard_map/ppermute | solution.py:306
  43.3 0.0 collective-permute-done.13
  43.3 1.4 %collective-permute-start.14 = (f32[32,640]{1,0:T(8,128)S(1)}, f32[32,640]{1,0:T(8,128)S(1)}, u32[]{:S(2)}, u32[]{:S(2)}) collective-permute-start(f32[32,640]{1,0:T(8,128)S(1)} %add.59), channel_id=1, source_target_pairs={{0,16},{1,17},{2,18},{3,19},{4,20},{5,21},{6,22},{7,23},{8,24},{9,... | collective-permute-start | bytes 245768 | tf_op jit(solution)/shard_map/ppermute | solution.py:306
  44.7 1.1 %collective-permute-done.7 = f32[32,384]{1,0:T(8,128)S(1)} collective-permute-done((f32[32,384]{1,0:T(8,128)S(1)}, f32[32,384]{1,0:T(8,128)S(1)}, u32[]{:S(2)}, u32[]{:S(2)}) %collective-permute-start.7) | collective-permute-done | bytes 49184 | tf_op jit(solution)/shard_map/ppermute | solution.py:306
  45.8 1.5 %collective-permute-start.8 = (f32[32,384]{1,0:T(8,128)S(1)}, f32[32,384]{1,0:T(8,128)S(1)}, u32[]{:S(2)}, u32[]{:S(2)}) collective-permute-start(f32[32,384]{1,0:T(8,128)S(1)} %slice_add_fusion.1), channel_id=1, source_target_pairs={{0,1},{1,0},{2,3},{3,2},{4,5},{5,4},{6,7},{7,6},{8,9},{9,8},{10,11... | collective-permute-start | bytes 147464 | tf_op jit(solution)/shard_map/ppermute | solution.py:306
  47.4 0.4 collective-permute-done.14
  47.8 0.1 collective-permute-start.17
  47.9 2.1 %collective-permute-done.8 = f32[32,384]{1,0:T(8,128)S(1)} collective-permute-done((f32[32,384]{1,0:T(8,128)S(1)}, f32[32,384]{1,0:T(8,128)S(1)}, u32[]{:S(2)}, u32[]{:S(2)}) %collective-permute-start.8) | collective-permute-done | bytes 49184 | tf_op jit(solution)/shard_map/ppermute | solution.py:306
  50.0 0.1 collective-permute-start.16
  50.1 2.3 %factor.2.work = f32[64,128]{1,0:T(8,128)S(1)} custom-call(f32[32,512]{1,0:T(8,128)S(1)} %add.53.packed), custom_call_target="tpu_custom_call" | custom-call | flops 524288 | bytes 32768 | tf_op jit(solution)/shard_map/factor/pallas_call | solution.py:211
  52.4 2.1 %factor.3.refs_0_ = f32[64,64]{1,0:T(8,128)S(1)} custom-call(f32[64,128]{1,0:T(8,128)S(1)} %factor.2.work), custom_call_target="tpu_custom_call" | custom-call | flops 524288 | bytes 32768 | tf_op jit(solution)/shard_map/factor/pallas_call | solution.py:211
  54.4 0.5 collective-permute-start.15
  55.0 0.9 %collective-permute-done.15.refs_6_ = f32[64,64]{1,0:T(8,128)S(1)} collective-permute-done((f32[64,64]{1,0:T(8,128)S(1)}, f32[64,64]{1,0:T(8,128)S(1)}, u32[]{:S(2)}, u32[]{:S(2)}) %collective-permute-start.15) | collective-permute-done | bytes 16416 | tf_op jit(solution)/shard_map/ppermute | solution.py:306
  55.8 0.0 collective-permute-done.16.refs_10_
  55.8 0.0 collective-permute-done.17.refs_11_
  55.8 6.4 %final.1 = (bf16[2,1024,1024]{2,1,0:T(8,128)(2,1)}, f32[1,2,1024,1024]{3,2,1,0:T(8,128)}, f32[2,64,1024]{2,1,0:T(8,128)}) custom-call(s32[1]{0:T(128)} %bitcast.code, f32[64,64]{1,0:T(8,128)S(1)} %factor.3.refs_0_, f32[64,1024]{1,0:T(8,128)S(1)} %add_multiply_fusion.left.refs_1_, bf16[1024,1024]{1,0:T(8,128)(2,1)S(1)} %get-tuple-element.17.high.refs_2_, ...), custom_call_target="tpu_custom_call" | custom-call | flops 805306368 | bytes 20971520 | tf_op jit(solution)/shard_map/final/pallas_call | solution.py:265
  (18 shorter events, 0.2 us)
Async XLA Ops:
  6.4 1.7 %collective-permute-start = (f32[64,1024]{1,0:T(8,128)S(1)}, f32[64,1024]{1,0:T(8,128)S(1)}, u32[]{:S(2)}, u32[]{:S(2)}) collective-permute-start(f32[64,1024]{1,0:T(8,128)S(1)} %get-tuple-element.16), channel_id=1, source_target_pairs={{0,8},{1,9},{2,10},{3,11},{4,12},{5,13},{6,14},{7,15},{8,0},{9,1},... | collective-permute-start | bytes 786440 | tf_op jit(solution)/shard_map/ppermute | solution.py:306
  8.2 9.6 %collective-permute-start.1 = (f32[64,1024]{1,0:T(8,128)S(1)}, f32[64,1024]{1,0:T(8,128)S(1)}, u32[]{:S(2)}, u32[]{:S(2)}) collective-permute-start(f32[64,1024]{1,0:T(8,128)S(1)} %add.48), channel_id=1, source_target_pairs={{0,16},{1,17},{2,18},{3,19},{4,20},{5,21},{6,22},{7,23},{8,24},{9,... | collective-permute-start | bytes 786440 | tf_op jit(solution)/shard_map/ppermute | solution.py:306
  17.8 1.6 %collective-permute-start.2 = (f32[64,1024]{1,0:T(8,128)S(1)}, f32[64,1024]{1,0:T(8,128)S(1)}, u32[]{:S(2)}, u32[]{:S(2)}) collective-permute-start(f32[64,1024]{1,0:T(8,128)S(1)} %add_multiply_fusion.left.refs_1_), channel_id=1, source_target_pairs={{0,8},{1,9},{2,10},{3,11},{4,12},{5,13},{6,14},{7,15},{8,0},{9,1},... | collective-permute-start | bytes 786440 | tf_op jit(solution)/shard_map/ppermute | solution.py:306
  19.8 2.4 %collective-permute-start.3 = (f32[64,384]{1,0:T(8,128)S(1)}, f32[64,384]{1,0:T(8,128)S(1)}, u32[]{:S(2)}, u32[]{:S(2)}) collective-permute-start(f32[64,384]{1,0:T(8,128)S(1)} %right.4), channel_id=1, source_target_pairs={{0,8},{1,9},{2,10},{3,11},{4,12},{5,13},{6,14},{7,15},{8,0},{9,1},... | collective-permute-start | bytes 294920 | tf_op jit(solution)/shard_map/ppermute | solution.py:306
  21.7 1.5 %collective-permute-start.9 = (f32[64,640]{1,0:T(8,128)S(1)}, f32[64,640]{1,0:T(8,128)S(1)}, u32[]{:S(2)}, u32[]{:S(2)}) collective-permute-start(f32[64,640]{1,0:T(8,128)S(1)} %right.5), channel_id=1, source_target_pairs={{0,8},{1,9},{2,10},{3,11},{4,12},{5,13},{6,14},{7,15},{8,0},{9,1},... | collective-permute-start | bytes 491528 | tf_op jit(solution)/shard_map/ppermute | solution.py:306
  23.2 4.8 %collective-permute-start.10 = (f32[32,640]{1,0:T(8,128)S(1)}, f32[32,640]{1,0:T(8,128)S(1)}, u32[]{:S(2)}, u32[]{:S(2)}) collective-permute-start(f32[32,640]{1,0:T(8,128)S(1)} %slice.24), channel_id=1, source_target_pairs={{0,16},{1,17},{2,18},{3,19},{4,20},{5,21},{6,22},{7,23},{8,24},{9,... | collective-permute-start | bytes 245768 | tf_op jit(solution)/shard_map/ppermute | solution.py:306
  25.1 4.8 %collective-permute-start.4 = (f32[32,512]{1,0:T(8,128)S(1)}, f32[32,512]{1,0:T(8,128)S(1)}, u32[]{:S(2)}, u32[]{:S(2)}) collective-permute-start(f32[32,512]{1,0:T(8,128)S(1)} %pad_maximum_fusion.2), channel_id=1, source_target_pairs={{0,1},{1,0},{2,3},{3,2},{4,5},{5,4},{6,7},{7,6},{8,9},{9,8},{10,11... | collective-permute-start | bytes 196616 | tf_op jit(solution)/shard_map/ppermute | solution.py:306
  28.0 4.5 %collective-permute-start.11 = (f32[32,640]{1,0:T(8,128)S(1)}, f32[32,640]{1,0:T(8,128)S(1)}, u32[]{:S(2)}, u32[]{:S(2)}) collective-permute-start(f32[32,640]{1,0:T(8,128)S(1)} %slice_add_fusion), channel_id=1, source_target_pairs={{0,1},{1,0},{2,3},{3,2},{4,5},{5,4},{6,7},{7,6},{8,9},{9,8},{10,11... | collective-permute-start | bytes 245768 | tf_op jit(solution)/shard_map/ppermute | solution.py:306
  29.8 4.9 %collective-permute-start.5 = (f32[32,512]{1,0:T(8,128)S(1)}, f32[32,512]{1,0:T(8,128)S(1)}, u32[]{:S(2)}, u32[]{:S(2)}) collective-permute-start(f32[32,512]{1,0:T(8,128)S(1)} %fusion), channel_id=1, source_target_pairs={{0,2},{1,3},{2,0},{3,1},{4,6},{5,7},{6,4},{7,5},{8,10},{9,11},{10,... | collective-permute-start | bytes 196616 | tf_op jit(solution)/shard_map/ppermute | solution.py:306
  32.6 5.1 %collective-permute-start.12 = (f32[32,640]{1,0:T(8,128)S(1)}, f32[32,640]{1,0:T(8,128)S(1)}, u32[]{:S(2)}, u32[]{:S(2)}) collective-permute-start(f32[32,640]{1,0:T(8,128)S(1)} %add.57), channel_id=1, source_target_pairs={{0,2},{1,3},{2,0},{3,1},{4,6},{5,7},{6,4},{7,5},{8,10},{9,11},{10,... | collective-permute-start | bytes 245768 | tf_op jit(solution)/shard_map/ppermute | solution.py:306
  34.7 7.0 %collective-permute-start.6 = (f32[32,512]{1,0:T(8,128)S(1)}, f32[32,512]{1,0:T(8,128)S(1)}, u32[]{:S(2)}, u32[]{:S(2)}) collective-permute-start(f32[32,512]{1,0:T(8,128)S(1)} %add.52), channel_id=1, source_target_pairs={{0,4},{1,5},{2,6},{3,7},{4,0},{5,1},{6,2},{7,3},{8,12},{9,13},{10,... | collective-permute-start | bytes 196616 | tf_op jit(solution)/shard_map/ppermute | solution.py:306
  37.7 5.6 %collective-permute-start.13 = (f32[32,640]{1,0:T(8,128)S(1)}, f32[32,640]{1,0:T(8,128)S(1)}, u32[]{:S(2)}, u32[]{:S(2)}) collective-permute-start(f32[32,640]{1,0:T(8,128)S(1)} %add.58), channel_id=1, source_target_pairs={{0,4},{1,5},{2,6},{3,7},{4,0},{5,1},{6,2},{7,3},{8,12},{9,13},{10,... | collective-permute-start | bytes 245768 | tf_op jit(solution)/shard_map/ppermute | solution.py:306
  41.7 4.2 %collective-permute-start.7 = (f32[32,384]{1,0:T(8,128)S(1)}, f32[32,384]{1,0:T(8,128)S(1)}, u32[]{:S(2)}, u32[]{:S(2)}) collective-permute-start(f32[32,384]{1,0:T(8,128)S(1)} %slice.22), channel_id=1, source_target_pairs={{0,16},{1,17},{2,18},{3,19},{4,20},{5,21},{6,22},{7,23},{8,24},{9,... | collective-permute-start | bytes 147464 | tf_op jit(solution)/shard_map/ppermute | solution.py:306
  43.3 4.5 %collective-permute-start.14 = (f32[32,640]{1,0:T(8,128)S(1)}, f32[32,640]{1,0:T(8,128)S(1)}, u32[]{:S(2)}, u32[]{:S(2)}) collective-permute-start(f32[32,640]{1,0:T(8,128)S(1)} %add.59), channel_id=1, source_target_pairs={{0,16},{1,17},{2,18},{3,19},{4,20},{5,21},{6,22},{7,23},{8,24},{9,... | collective-permute-start | bytes 245768 | tf_op jit(solution)/shard_map/ppermute | solution.py:306
  45.8 4.2 %collective-permute-start.8 = (f32[32,384]{1,0:T(8,128)S(1)}, f32[32,384]{1,0:T(8,128)S(1)}, u32[]{:S(2)}, u32[]{:S(2)}) collective-permute-start(f32[32,384]{1,0:T(8,128)S(1)} %slice_add_fusion.1), channel_id=1, source_target_pairs={{0,1},{1,0},{2,3},{3,2},{4,5},{5,4},{6,7},{7,6},{8,9},{9,8},{10,11... | collective-permute-start | bytes 147464 | tf_op jit(solution)/shard_map/ppermute | solution.py:306
  47.8 8.0 %collective-permute-start.17 = (f32[64,640]{1,0:T(8,128)S(1)}, f32[64,640]{1,0:T(8,128)S(1)}, u32[]{:S(2)}, u32[]{:S(2)}) collective-permute-start(f32[64,640]{1,0:T(8,128)S(1)} %pad_maximum_fusion.refs_5_), channel_id=1, source_target_pairs={{0,8},{1,9},{2,10},{3,11},{4,12},{5,13},{6,14},{7,15},{8,0},{9,1},... | collective-permute-start | bytes 491528 | tf_op jit(solution)/shard_map/ppermute | solution.py:306
  50.0 5.8 %collective-permute-start.16 = (f32[64,384]{1,0:T(8,128)S(1)}, f32[64,384]{1,0:T(8,128)S(1)}, u32[]{:S(2)}, u32[]{:S(2)}) collective-permute-start(f32[64,384]{1,0:T(8,128)S(1)} %pad_maximum_fusion.1.refs_4_), channel_id=1, source_target_pairs={{0,8},{1,9},{2,10},{3,11},{4,12},{5,13},{6,14},{7,15},{8,0},{9,1},... | collective-permute-start | bytes 294920 | tf_op jit(solution)/shard_map/ppermute | solution.py:306
  54.4 1.4 %collective-permute-start.15 = (f32[64,64]{1,0:T(8,128)S(1)}, f32[64,64]{1,0:T(8,128)S(1)}, u32[]{:S(2)}, u32[]{:S(2)}) collective-permute-start(f32[64,64]{1,0:T(8,128)S(1)} %factor.3.refs_0_), channel_id=1, source_target_pairs={{0,8},{1,9},{2,10},{3,11},{4,12},{5,13},{6,14},{7,15},{8,0},{9,1},... | collective-permute-start | bytes 49160 | tf_op jit(solution)/shard_map/ppermute | solution.py:306

commit v2 on v1

--- a/solution.py
+++ b/solution.py
@@ -221,51 +221,83 @@
     )(array)
 
 
+def prepare(code, keeps, scale, inverse, left, totals):
+    rights = [
+        dot(inverse[...], ordered(total, 1 - bit(code, keep)) * scale, NN, HIGHEST)
+        for keep, total in zip(keeps, totals)
+    ]
+    right = jnp.concatenate(rights, axis=1)
+    top, rest = split(right)
+    pieces = jnp.concatenate([top, rest, top], axis=0)
+    top, rest = split(dot(left[...], inverse[...], TT, HIGHEST))
+    return right, pieces, jnp.concatenate([top, top, rest], axis=1)
+
+
+def prepare_kernel(keeps, scale, code, inverse, left, *refs):
+    outs = prepare(code, keeps, scale, inverse, left, refs[:-3])
+    for ref, value in zip(refs[-3:], outs):
+        ref[...] = value
+
+
+def prepare_of(keeps, code, scale, inverse, left, *totals):
+    rank, rows = left.shape
+    cols = sum(total.shape[1] for total in totals)
+    return pl.pallas_call(
+        functools.partial(prepare_kernel, keeps, scale),
+        name="prepare",
+        in_specs=[SMEM] + [VMEM] * (2 + len(totals)),
+        out_specs=[VMEM] * 3,
+        out_shape=[
+            shape_of(rank, cols),
+            shape_of(3 * rank, cols, dtype=BF16),
+            shape_of(rows, 3 * rank, dtype=BF16),
+        ],
+        compiler_params=params(8),
+        cost_estimate=pl.CostEstimate(
+            flops=24 * rank * rank * cols, bytes_accessed=20 * rank * cols, transcendentals=0
+        ),
+    )(code, inverse, left, *totals)
+
+
 def final_kernel(block, scale, keeps, code, *refs):
     update, new_error, basis_next, updates, errors, rights, sems = refs[-7:]
-    count = (len(refs) - 7) // 2
+    right_m, pieces_m, ortho_m, high_m, low_m, inverse_t, left_t, high_t, low_t, *totals_t = refs[:-7]
+    rows = high_m.shape[0]
     copies = []
+
+    def send(which, kind, i, source, target):
+        copies.append(pltpu.make_async_copy(source, target, sems.at[which, kind, i]))
+        copies[-1].start()
+
     for which in range(2):
-        inverse, left, high, low, *totals = refs[count * which : count * (which + 1)]
-        rows = left.shape[1]
         w = bit(code, which)
-        start = 0
-        pieces = []
-        for keep, total in zip(keeps, totals):
-            columns = slice(start, start + total.shape[1])
-            right = dot(inverse[...], ordered(total, 1 - bit(code, keep)) * scale, NN, HIGHEST)
-            rights[which, :, columns] = right
-            top, rest = split(right)
-            pieces.append(jnp.concatenate([top, rest, top], axis=0))
-            start += total.shape[1]
-        pieces = jnp.concatenate(pieces, axis=1)
-        copies.append(pltpu.make_async_copy(rights.at[which], basis_next.at[w], sems.at[which, 2, 0]))
-        copies[-1].start()
-        top, rest = split(dot(left[...], inverse[...], TT, HIGHEST))
-        ortho = jnp.concatenate([top, top, rest], axis=1)
+        if which == 0:
+            pieces, ortho, high, low = pieces_m[...], ortho_m, high_m, low_m
+            send(which, 2, 0, right_m, basis_next.at[w])
+        else:
+            right, pieces, ortho = prepare(code, keeps, scale, inverse_t, left_t, totals_t)
+            high, low = high_t, low_t
+            rights[...] = right
+            send(which, 2, 0, rights, basis_next.at[w])
         for i, start in enumerate(range(0, rows, block)):
             part, where = slice(start, start + block), pl.ds(start, block)
             approx = dot(ortho[part], pieces, NN)
             updates[which, part] = approx.astype(BF16)
             errors[which, part] = (high[part].astype(F32) + low[part].astype(F32)) - approx
-            for kind, source, target in (
-                (0, errors.at[which, where], new_error.at[0, w, where]),
-                (1, updates.at[which, where], update.at[w, where]),
-            ):
-                copies.append(pltpu.make_async_copy(source, target, sems.at[which, kind, i]))
-                copies[-1].start()
+            send(which, 0, i, errors.at[which, where], new_error.at[0, w, where])
+            send(which, 1, i, updates.at[which, where], update.at[w, where])
     for copy in copies:
         copy.wait()
 
 
 def final_of(keeps, code, mine, theirs, scale):
-    rank, rows = mine[1].shape
-    cols = mine[2].shape[1]
+    rank = mine[0].shape[0]
+    rows, cols = mine[3].shape
     block = min(rows, FINAL_ROWS)
     return pl.pallas_call(
         functools.partial(final_kernel, block, scale, keeps),
         name="final",
-        in_specs=[SMEM] + [VMEM] * (2 * len(mine)),
+        in_specs=[SMEM] + [VMEM] * (len(mine) + len(theirs)),
         out_specs=[ANY] * 3,
         out_shape=[
             shape_of(2, rows, cols, dtype=BF16),
@@ -275,7 +307,7 @@
         scratch_shapes=[
             pltpu.VMEM((2, rows, cols), BF16),
             pltpu.VMEM((2, rows, cols), F32),
-            pltpu.VMEM((2, rank, cols), F32),
+            pltpu.VMEM((rank, cols), F32),
             pltpu.SemaphoreType.DMA((2, 3, rows // block)),
         ],
         compiler_params=params(24),
@@ -362,12 +394,14 @@
         total = jnp.concatenate([stay, back], axis=0)
         totals_m.append(total)
         totals_t.append(core(total))
-    inverse_t = core(inverse_m)
-
+        if part == 0:
+            inverse_t = core(inverse_m)
+
+    ready = prepare_of(keeps, code, scale, inverse_m, left_m, *totals_m)
     update, new_error, right = final_of(
         keeps,
         code,
-        (inverse_m, left_m, high_m, low_m, *totals_m),
+        (*ready, high_m, low_m),
         (inverse_t, left_t, high_t, low_t, *totals_t),
         scale,
     )

time: 62.4 us -> 61.3 us (0.982)
  waiting for transfers between devices: 19.9 us -> 19 us
    pallas_call x1, Pallas kernels: 6.39 us -> 5.29 us  [final_of(): pl.pallas_call(functools.partial(final_kernel, block, scale, keeps), name...]
    pallas_call x0 -> x1, Pallas kernels: none -> 0.87 us  [prepare_of(): pl.pallas_call(functools.partial(prepare_kernel, keeps, scale), name='pre...]
    ppermute x18, waiting for transfers between devices: 19.9 us -> 19 us  [swap(): return lax.ppermute(value, AXES, pairs)]
  transfers between devices with their start and end apart: 18 -> 18, of which waited for: 13 -> 12; matrix products, arithmetic and copies ran while one was open for 0% -> 0% of each run, Pallas kernels for 10% -> 11%
where the time goes in v2:
time: 61.3 us; the launch traced here: 61.1 us
  starting transfers between devices  22.7 us (37%)
  waiting for transfers between devices  19 us (31%)
  Pallas kernels  18.4 us (30%)
  between operations  0.81 us (1%)
    ppermute x18, starting transfers between devices, swap(): return lax.ppermute(value, AXES, pairs)  22.7 us
    ppermute x18, waiting for transfers between devices, swap(): return lax.ppermute(value, AXES, pairs)  19 us
    pallas_call x1, Pallas kernels, left_of(): pl.pallas_call(functools.partial(left_kernel, block, jobs), name='left',...  5.8 us
    pallas_call x1, Pallas kernels, final_of(): pl.pallas_call(functools.partial(final_kernel, block, scale, keeps), name...  5.29 us
    pallas_call x2, Pallas kernels, factor_of(): pl.pallas_call(kernel, name='factor', in_specs=[VMEM], out_specs=VMEM, ou...  4.35 us
    pallas_call x3, Pallas kernels, right_of(): pl.pallas_call(functools.partial(right_kernel, [start for start, _ in col...  2.13 us
  transfers between devices with their start and end apart: 18, of which 12 were waited for; matrix products, arithmetic and copies ran while one was open for 0% of the time, Pallas kernels for 11%

profile of v2, /device:TPU:0, one launch (start us, length us, event | category | flops | bytes accessed | tf_op | source)
XLA Modules:
  0.0 61.1 jit_solution(15053693278700455532)
XLA Ops:
  0.6 5.8 %left.1 = (bf16[1024,1024]{1,0:T(8,128)(2,1)S(1)}, bf16[1024,1024]{1,0:T(8,128)(2,1)S(1)}, f32[64,1024]{1,0:T(8,128)S(1)}, bf16[1024,1024]{1,0:T(8,128)(2,1)S(1)...) custom-call(s32[1]{0:T(128)} %bitcast.code, bf16[1,2,1024,1024]{3,2,1,0:T(8,128)(2,1)} %grad.1, ...), custom_call_target="tpu_custom_call" | custom-call | flops 805306368 | bytes 20971520 | tf_op jit(solution)/shard_map/left/pallas_call | solution.py:94
  6.4 0.6 collective-permute-start
  7.0 1.2 %collective-permute-done = f32[64,1024]{1,0:T(8,128)S(1)} collective-permute-done((f32[64,1024]{1,0:T(8,128)S(1)}, f32[64,1024]{1,0:T(8,128)S(1)}, u32[]{:S(2)}, u32[]{:S(2)}) %collective-permute-start) | collective-permute-done | bytes 262176 | tf_op jit(solution)/shard_map/ppermute | solution.py:338
  8.2 3.0 %collective-permute-start.1 = (f32[64,1024]{1,0:T(8,128)S(1)}, f32[64,1024]{1,0:T(8,128)S(1)}, u32[]{:S(2)}, u32[]{:S(2)}) collective-permute-start(f32[64,1024]{1,0:T(8,128)S(1)} %add.48), channel_id=1, source_target_pairs={{0,16},{1,17},{2,18},{3,19},{4,20},{5,21},{6,22},{7,23},{8,24},{9,... | collective-permute-start | bytes 786440 | tf_op jit(solution)/shard_map/ppermute | solution.py:338
  11.1 6.6 %collective-permute-done.1 = f32[64,1024]{1,0:T(8,128)S(1)} collective-permute-done((f32[64,1024]{1,0:T(8,128)S(1)}, f32[64,1024]{1,0:T(8,128)S(1)}, u32[]{:S(2)}, u32[]{:S(2)}) %collective-permute-start.1) | collective-permute-done | bytes 262176 | tf_op jit(solution)/shard_map/ppermute | solution.py:338
  17.8 0.1 collective-permute-start.2
  17.9 1.5 %collective-permute-done.2.left.refs_6_ = f32[64,1024]{1,0:T(8,128)S(1)} collective-permute-done((f32[64,1024]{1,0:T(8,128)S(1)}, f32[64,1024]{1,0:T(8,128)S(1)}, u32[]{:S(2)}, u32[]{:S(2)}) %collective-permute-start.2) | collective-permute-done | bytes 262176 | tf_op jit(solution)/shard_map/ppermute | solution.py:338
  19.4 0.4 right.4
  19.8 0.2 collective-permute-start.3
  20.0 1.1 %right.3 = (f32[64,384]{1,0:T(8,128)S(1)}, f32[64,640]{1,0:T(8,128)S(1)}, f32[32,128]{1,0:T(8,128)S(1)}) custom-call(s32[1]{0:T(128)} %bitcast.code, f32[64,1024]{1,0:T(8,128)S(1)} %add_multiply_fusion.left, bf16[1024,1024]{1,0:T(8,128)(2,1)S(1)} %get-tuple-element.20.high.refs_3_, bf16[1024,1024]{1,0:T(8,128)(2,1)S(1)} %get-tuple-element.21.low.refs_4_), custom_call_target="tpu_custom_call" | custom-call | flops 402653184 | bytes 4194304 | tf_op jit(solution)/shard_map/right/pallas_call | solution.py:149
  21.1 0.6 %right.5 = f32[64,640]{1,0:T(8,128)S(1)} custom-call(s32[1]{0:T(128)} %bitcast.code, f32[64,1024]{1,0:T(8,128)S(1)} %collective-permute-done.2.left.refs_6_, bf16[1024,1024]{1,0:T(8,128)(2,1)S(1)} %get-tuple-element.23.high.refs_7_, bf16[1024,1024]{1,0:T(8,128)(2,1)S(1)} %get-tuple-element.24.low.refs_8_), custom_call_target="tpu_custom_call" | custom-call | flops 251658240 | bytes 2621440 | tf_op jit(solution)/shard_map/right/pallas_call | solution.py:149
  21.7 0.4 collective-permute-start.9
  22.2 0.0 collective-permute-done.3
  22.2 1.0 %collective-permute-done.9 = f32[64,640]{1,0:T(8,128)S(1)} collective-permute-done((f32[64,640]{1,0:T(8,128)S(1)}, f32[64,640]{1,0:T(8,128)S(1)}, u32[]{:S(2)}, u32[]{:S(2)}) %collective-permute-start.9) | collective-permute-done | bytes 163872 | tf_op jit(solution)/shard_map/ppermute | solution.py:338
  23.2 1.8 %collective-permute-start.10 = (f32[32,640]{1,0:T(8,128)S(1)}, f32[32,640]{1,0:T(8,128)S(1)}, u32[]{:S(2)}, u32[]{:S(2)}) collective-permute-start(f32[32,640]{1,0:T(8,128)S(1)} %slice.24), channel_id=1, source_target_pairs={{0,16},{1,17},{2,18},{3,19},{4,20},{5,21},{6,22},{7,23},{8,24},{9,... | collective-permute-start | bytes 245768 | tf_op jit(solution)/shard_map/ppermute | solution.py:338
  25.1 1.5 %collective-permute-start.4 = (f32[32,512]{1,0:T(8,128)S(1)}, f32[32,512]{1,0:T(8,128)S(1)}, u32[]{:S(2)}, u32[]{:S(2)}) collective-permute-start(f32[32,512]{1,0:T(8,128)S(1)} %pad_maximum_fusion.2), channel_id=1, source_target_pairs={{0,1},{1,0},{2,3},{3,2},{4,5},{5,4},{6,7},{7,6},{8,9},{9,8},{10,11... | collective-permute-start | bytes 196616 | tf_op jit(solution)/shard_map/ppermute | solution.py:338
  26.5 1.5 %collective-permute-done.10 = f32[32,640]{1,0:T(8,128)S(1)} collective-permute-done((f32[32,640]{1,0:T(8,128)S(1)}, f32[32,640]{1,0:T(8,128)S(1)}, u32[]{:S(2)}, u32[]{:S(2)}) %collective-permute-start.10) | collective-permute-done | bytes 81952 | tf_op jit(solution)/shard_map/ppermute | solution.py:338
  28.0 1.8 %collective-permute-start.11 = (f32[32,640]{1,0:T(8,128)S(1)}, f32[32,640]{1,0:T(8,128)S(1)}, u32[]{:S(2)}, u32[]{:S(2)}) collective-permute-start(f32[32,640]{1,0:T(8,128)S(1)} %slice_add_fusion), channel_id=1, source_target_pairs={{0,1},{1,0},{2,3},{3,2},{4,5},{5,4},{6,7},{7,6},{8,9},{9,8},{10,11... | collective-permute-start | bytes 245768 | tf_op jit(solution)/shard_map/ppermute | solution.py:338
  29.8 0.0 collective-permute-done.4
  29.8 1.6 %collective-permute-start.5 = (f32[32,512]{1,0:T(8,128)S(1)}, f32[32,512]{1,0:T(8,128)S(1)}, u32[]{:S(2)}, u32[]{:S(2)}) collective-permute-start(f32[32,512]{1,0:T(8,128)S(1)} %fusion), channel_id=1, source_target_pairs={{0,2},{1,3},{2,0},{3,1},{4,6},{5,7},{6,4},{7,5},{8,10},{9,11},{10,... | collective-permute-start | bytes 196616 | tf_op jit(solution)/shard_map/ppermute | solution.py:338
  31.5 1.1 %collective-permute-done.11 = f32[32,640]{1,0:T(8,128)S(1)} collective-permute-done((f32[32,640]{1,0:T(8,128)S(1)}, f32[32,640]{1,0:T(8,128)S(1)}, u32[]{:S(2)}, u32[]{:S(2)}) %collective-permute-start.11) | collective-permute-done | bytes 81952 | tf_op jit(solution)/shard_map/ppermute | solution.py:338
  32.6 1.9 %collective-permute-start.12 = (f32[32,640]{1,0:T(8,128)S(1)}, f32[32,640]{1,0:T(8,128)S(1)}, u32[]{:S(2)}, u32[]{:S(2)}) collective-permute-start(f32[32,640]{1,0:T(8,128)S(1)} %add.57), channel_id=1, source_target_pairs={{0,2},{1,3},{2,0},{3,1},{4,6},{5,7},{6,4},{7,5},{8,10},{9,11},{10,... | collective-permute-start | bytes 245768 | tf_op jit(solution)/shard_map/ppermute | solution.py:338
  34.4 0.3 collective-permute-done.5
  34.7 2.5 %collective-permute-start.6 = (f32[32,512]{1,0:T(8,128)S(1)}, f32[32,512]{1,0:T(8,128)S(1)}, u32[]{:S(2)}, u32[]{:S(2)}) collective-permute-start(f32[32,512]{1,0:T(8,128)S(1)} %add.52), channel_id=1, source_target_pairs={{0,4},{1,5},{2,6},{3,7},{4,0},{5,1},{6,2},{7,3},{8,12},{9,13},{10,... | collective-permute-start | bytes 196616 | tf_op jit(solution)/shard_map/ppermute | solution.py:338
  37.2 0.5 collective-permute-done.12
  37.7 2.2 %collective-permute-start.13 = (f32[32,640]{1,0:T(8,128)S(1)}, f32[32,640]{1,0:T(8,128)S(1)}, u32[]{:S(2)}, u32[]{:S(2)}) collective-permute-start(f32[32,640]{1,0:T(8,128)S(1)} %add.58), channel_id=1, source_target_pairs={{0,4},{1,5},{2,6},{3,7},{4,0},{5,1},{6,2},{7,3},{8,12},{9,13},{10,... | collective-permute-start | bytes 245768 | tf_op jit(solution)/shard_map/ppermute | solution.py:338
  39.9 1.7 %collective-permute-done.6 = f32[32,512]{1,0:T(8,128)S(1)} collective-permute-done((f32[32,512]{1,0:T(8,128)S(1)}, f32[32,512]{1,0:T(8,128)S(1)}, u32[]{:S(2)}, u32[]{:S(2)}) %collective-permute-start.6) | collective-permute-done | bytes 65568 | tf_op jit(solution)/shard_map/ppermute | solution.py:338
  41.7 1.6 %collective-permute-start.7 = (f32[32,384]{1,0:T(8,128)S(1)}, f32[32,384]{1,0:T(8,128)S(1)}, u32[]{:S(2)}, u32[]{:S(2)}) collective-permute-start(f32[32,384]{1,0:T(8,128)S(1)} %slice.22), channel_id=1, source_target_pairs={{0,16},{1,17},{2,18},{3,19},{4,20},{5,21},{6,22},{7,23},{8,24},{9,... | collective-permute-start | bytes 147464 | tf_op jit(solution)/shard_map/ppermute | solution.py:338
  43.3 0.0 collective-permute-done.13
  43.3 1.4 %collective-permute-start.14 = (f32[32,640]{1,0:T(8,128)S(1)}, f32[32,640]{1,0:T(8,128)S(1)}, u32[]{:S(2)}, u32[]{:S(2)}) collective-permute-start(f32[32,640]{1,0:T(8,128)S(1)} %add.59), channel_id=1, source_target_pairs={{0,16},{1,17},{2,18},{3,19},{4,20},{5,21},{6,22},{7,23},{8,24},{9,... | collective-permute-start | bytes 245768 | tf_op jit(solution)/shard_map/ppermute | solution.py:338
  44.7 1.1 %collective-permute-done.7 = f32[32,384]{1,0:T(8,128)S(1)} collective-permute-done((f32[32,384]{1,0:T(8,128)S(1)}, f32[32,384]{1,0:T(8,128)S(1)}, u32[]{:S(2)}, u32[]{:S(2)}) %collective-permute-start.7) | collective-permute-done | bytes 49184 | tf_op jit(solution)/shard_map/ppermute | solution.py:338
  45.8 1.5 %collective-permute-start.8 = (f32[32,384]{1,0:T(8,128)S(1)}, f32[32,384]{1,0:T(8,128)S(1)}, u32[]{:S(2)}, u32[]{:S(2)}) collective-permute-start(f32[32,384]{1,0:T(8,128)S(1)} %slice_add_fusion.1), channel_id=1, source_target_pairs={{0,1},{1,0},{2,3},{3,2},{4,5},{5,4},{6,7},{7,6},{8,9},{9,8},{10,11... | collective-permute-start | bytes 147464 | tf_op jit(solution)/shard_map/ppermute | solution.py:338
  47.4 0.4 collective-permute-done.14
  47.8 0.1 collective-permute-start.17
  47.9 2.1 %collective-permute-done.8 = f32[32,384]{1,0:T(8,128)S(1)} collective-permute-done((f32[32,384]{1,0:T(8,128)S(1)}, f32[32,384]{1,0:T(8,128)S(1)}, u32[]{:S(2)}, u32[]{:S(2)}) %collective-permute-start.8) | collective-permute-done | bytes 49184 | tf_op jit(solution)/shard_map/ppermute | solution.py:338
  50.0 0.1 collective-permute-start.16
  50.1 2.3 %factor.2.work = f32[64,128]{1,0:T(8,128)S(1)} custom-call(f32[32,512]{1,0:T(8,128)S(1)} %add.53.packed), custom_call_target="tpu_custom_call" | custom-call | flops 524288 | bytes 32768 | tf_op jit(solution)/shard_map/factor/pallas_call | solution.py:211
  52.4 2.1 %factor.3.inverse = f32[64,64]{1,0:T(8,128)S(1)} custom-call(f32[64,128]{1,0:T(8,128)S(1)} %factor.2.work), custom_call_target="tpu_custom_call" | custom-call | flops 524288 | bytes 32768 | tf_op jit(solution)/shard_map/factor/pallas_call | solution.py:211
  54.4 0.5 collective-permute-start.15
  55.0 0.9 %prepare.1 = (f32[64,1024]{1,0:T(8,128)S(1)}, bf16[192,1024]{1,0:T(8,128)(2,1)S(1)}, bf16[1024,192]{1,0:T(8,128)(2,1)S(1)}) custom-call(s32[1]{0:T(128)} %bitcast.code, f32[64,64]{1,0:T(8,128)S(1)} %factor.3.inverse, f32[64,1024]{1,0:T(8,128)S(1)} %add_multiply_fusion.left, f32[64,384]{1,0:T(8,128)S(1)} %pad_maximum_fusion.1.refs_0_, ...), custom_call_target="tpu_custom_call" | custom-call | flops 100663296 | bytes 1310720 | tf_op jit(solution)/shard_map/prepare/pallas_call | solution.py:245
  55.8 0.0 collective-permute-done.15.refs_5_
  55.8 0.0 collective-permute-done.16.refs_9_
  55.8 0.0 collective-permute-done.17.refs_10_
  55.9 5.3 %final.1 = (bf16[2,1024,1024]{2,1,0:T(8,128)(2,1)}, f32[1,2,1024,1024]{3,2,1,0:T(8,128)}, f32[2,64,1024]{2,1,0:T(8,128)}) custom-call(s32[1]{0:T(128)} %bitcast.code, f32[64,1024]{1,0:T(8,128)S(1)} %get-tuple-element.27.refs_0_, bf16[192,1024]{1,0:T(8,128)(2,1)S(1)} %get-tuple-element.28.refs_1_, bf16[1024,192]{1,0:T(8,128)(2,1)S(1)} %get-tuple-element.29.refs_2_, ...), custom_call_target="tpu_custom_call" | custom-call | flops 805306368 | bytes 20971520 | tf_op jit(solution)/shard_map/final/pallas_call | solution.py:297
  (18 shorter events, 0.2 us)
Async XLA Ops:
  6.4 1.7 %collective-permute-start = (f32[64,1024]{1,0:T(8,128)S(1)}, f32[64,1024]{1,0:T(8,128)S(1)}, u32[]{:S(2)}, u32[]{:S(2)}) collective-permute-start(f32[64,1024]{1,0:T(8,128)S(1)} %get-tuple-element.19), channel_id=1, source_target_pairs={{0,8},{1,9},{2,10},{3,11},{4,12},{5,13},{6,14},{7,15},{8,0},{9,1},... | collective-permute-start | bytes 786440 | tf_op jit(solution)/shard_map/ppermute | solution.py:338
  8.2 9.6 %collective-permute-start.1 = (f32[64,1024]{1,0:T(8,128)S(1)}, f32[64,1024]{1,0:T(8,128)S(1)}, u32[]{:S(2)}, u32[]{:S(2)}) collective-permute-start(f32[64,1024]{1,0:T(8,128)S(1)} %add.48), channel_id=1, source_target_pairs={{0,16},{1,17},{2,18},{3,19},{4,20},{5,21},{6,22},{7,23},{8,24},{9,... | collective-permute-start | bytes 786440 | tf_op jit(solution)/shard_map/ppermute | solution.py:338
  17.8 1.6 %collective-permute-start.2 = (f32[64,1024]{1,0:T(8,128)S(1)}, f32[64,1024]{1,0:T(8,128)S(1)}, u32[]{:S(2)}, u32[]{:S(2)}) collective-permute-start(f32[64,1024]{1,0:T(8,128)S(1)} %add_multiply_fusion.left), channel_id=1, source_target_pairs={{0,8},{1,9},{2,10},{3,11},{4,12},{5,13},{6,14},{7,15},{8,0},{9,1},... | collective-permute-start | bytes 786440 | tf_op jit(solution)/shard_map/ppermute | solution.py:338
  19.8 2.4 %collective-permute-start.3 = (f32[64,384]{1,0:T(8,128)S(1)}, f32[64,384]{1,0:T(8,128)S(1)}, u32[]{:S(2)}, u32[]{:S(2)}) collective-permute-start(f32[64,384]{1,0:T(8,128)S(1)} %right.4), channel_id=1, source_target_pairs={{0,8},{1,9},{2,10},{3,11},{4,12},{5,13},{6,14},{7,15},{8,0},{9,1},... | collective-permute-start | bytes 294920 | tf_op jit(solution)/shard_map/ppermute | solution.py:338
  21.7 1.5 %collective-permute-start.9 = (f32[64,640]{1,0:T(8,128)S(1)}, f32[64,640]{1,0:T(8,128)S(1)}, u32[]{:S(2)}, u32[]{:S(2)}) collective-permute-start(f32[64,640]{1,0:T(8,128)S(1)} %right.5), channel_id=1, source_target_pairs={{0,8},{1,9},{2,10},{3,11},{4,12},{5,13},{6,14},{7,15},{8,0},{9,1},... | collective-permute-start | bytes 491528 | tf_op jit(solution)/shard_map/ppermute | solution.py:338
  23.2 4.8 %collective-permute-start.10 = (f32[32,640]{1,0:T(8,128)S(1)}, f32[32,640]{1,0:T(8,128)S(1)}, u32[]{:S(2)}, u32[]{:S(2)}) collective-permute-start(f32[32,640]{1,0:T(8,128)S(1)} %slice.24), channel_id=1, source_target_pairs={{0,16},{1,17},{2,18},{3,19},{4,20},{5,21},{6,22},{7,23},{8,24},{9,... | collective-permute-start | bytes 245768 | tf_op jit(solution)/shard_map/ppermute | solution.py:338
  25.1 4.8 %collective-permute-start.4 = (f32[32,512]{1,0:T(8,128)S(1)}, f32[32,512]{1,0:T(8,128)S(1)}, u32[]{:S(2)}, u32[]{:S(2)}) collective-permute-start(f32[32,512]{1,0:T(8,128)S(1)} %pad_maximum_fusion.2), channel_id=1, source_target_pairs={{0,1},{1,0},{2,3},{3,2},{4,5},{5,4},{6,7},{7,6},{8,9},{9,8},{10,11... | collective-permute-start | bytes 196616 | tf_op jit(solution)/shard_map/ppermute | solution.py:338
  28.0 4.5 %collective-permute-start.11 = (f32[32,640]{1,0:T(8,128)S(1)}, f32[32,640]{1,0:T(8,128)S(1)}, u32[]{:S(2)}, u32[]{:S(2)}) collective-permute-start(f32[32,640]{1,0:T(8,128)S(1)} %slice_add_fusion), channel_id=1, source_target_pairs={{0,1},{1,0},{2,3},{3,2},{4,5},{5,4},{6,7},{7,6},{8,9},{9,8},{10,11... | collective-permute-start | bytes 245768 | tf_op jit(solution)/shard_map/ppermute | solution.py:338
  29.8 4.9 %collective-permute-start.5 = (f32[32,512]{1,0:T(8,128)S(1)}, f32[32,512]{1,0:T(8,128)S(1)}, u32[]{:S(2)}, u32[]{:S(2)}) collective-permute-start(f32[32,512]{1,0:T(8,128)S(1)} %fusion), channel_id=1, source_target_pairs={{0,2},{1,3},{2,0},{3,1},{4,6},{5,7},{6,4},{7,5},{8,10},{9,11},{10,... | collective-permute-start | bytes 196616 | tf_op jit(solution)/shard_map/ppermute | solution.py:338
  32.6 5.1 %collective-permute-start.12 = (f32[32,640]{1,0:T(8,128)S(1)}, f32[32,640]{1,0:T(8,128)S(1)}, u32[]{:S(2)}, u32[]{:S(2)}) collective-permute-start(f32[32,640]{1,0:T(8,128)S(1)} %add.57), channel_id=1, source_target_pairs={{0,2},{1,3},{2,0},{3,1},{4,6},{5,7},{6,4},{7,5},{8,10},{9,11},{10,... | collective-permute-start | bytes 245768 | tf_op jit(solution)/shard_map/ppermute | solution.py:338
  34.7 7.0 %collective-permute-start.6 = (f32[32,512]{1,0:T(8,128)S(1)}, f32[32,512]{1,0:T(8,128)S(1)}, u32[]{:S(2)}, u32[]{:S(2)}) collective-permute-start(f32[32,512]{1,0:T(8,128)S(1)} %add.52), channel_id=1, source_target_pairs={{0,4},{1,5},{2,6},{3,7},{4,0},{5,1},{6,2},{7,3},{8,12},{9,13},{10,... | collective-permute-start | bytes 196616 | tf_op jit(solution)/shard_map/ppermute | solution.py:338
  37.7 5.6 %collective-permute-start.13 = (f32[32,640]{1,0:T(8,128)S(1)}, f32[32,640]{1,0:T(8,128)S(1)}, u32[]{:S(2)}, u32[]{:S(2)}) collective-permute-start(f32[32,640]{1,0:T(8,128)S(1)} %add.58), channel_id=1, source_target_pairs={{0,4},{1,5},{2,6},{3,7},{4,0},{5,1},{6,2},{7,3},{8,12},{9,13},{10,... | collective-permute-start | bytes 245768 | tf_op jit(solution)/shard_map/ppermute | solution.py:338
  41.7 4.2 %collective-permute-start.7 = (f32[32,384]{1,0:T(8,128)S(1)}, f32[32,384]{1,0:T(8,128)S(1)}, u32[]{:S(2)}, u32[]{:S(2)}) collective-permute-start(f32[32,384]{1,0:T(8,128)S(1)} %slice.22), channel_id=1, source_target_pairs={{0,16},{1,17},{2,18},{3,19},{4,20},{5,21},{6,22},{7,23},{8,24},{9,... | collective-permute-start | bytes 147464 | tf_op jit(solution)/shard_map/ppermute | solution.py:338
  43.3 4.5 %collective-permute-start.14 = (f32[32,640]{1,0:T(8,128)S(1)}, f32[32,640]{1,0:T(8,128)S(1)}, u32[]{:S(2)}, u32[]{:S(2)}) collective-permute-start(f32[32,640]{1,0:T(8,128)S(1)} %add.59), channel_id=1, source_target_pairs={{0,16},{1,17},{2,18},{3,19},{4,20},{5,21},{6,22},{7,23},{8,24},{9,... | collective-permute-start | bytes 245768 | tf_op jit(solution)/shard_map/ppermute | solution.py:338
  45.8 4.2 %collective-permute-start.8 = (f32[32,384]{1,0:T(8,128)S(1)}, f32[32,384]{1,0:T(8,128)S(1)}, u32[]{:S(2)}, u32[]{:S(2)}) collective-permute-start(f32[32,384]{1,0:T(8,128)S(1)} %slice_add_fusion.1), channel_id=1, source_target_pairs={{0,1},{1,0},{2,3},{3,2},{4,5},{5,4},{6,7},{7,6},{8,9},{9,8},{10,11... | collective-permute-start | bytes 147464 | tf_op jit(solution)/shard_map/ppermute | solution.py:338
  47.8 8.0 %collective-permute-start.17 = (f32[64,640]{1,0:T(8,128)S(1)}, f32[64,640]{1,0:T(8,128)S(1)}, u32[]{:S(2)}, u32[]{:S(2)}) collective-permute-start(f32[64,640]{1,0:T(8,128)S(1)} %pad_maximum_fusion.refs_1_), channel_id=1, source_target_pairs={{0,8},{1,9},{2,10},{3,11},{4,12},{5,13},{6,14},{7,15},{8,0},{9,1},... | collective-permute-start | bytes 491528 | tf_op jit(solution)/shard_map/ppermute | solution.py:338
  50.0 5.8 %collective-permute-start.16 = (f32[64,384]{1,0:T(8,128)S(1)}, f32[64,384]{1,0:T(8,128)S(1)}, u32[]{:S(2)}, u32[]{:S(2)}) collective-permute-start(f32[64,384]{1,0:T(8,128)S(1)} %pad_maximum_fusion.1.refs_0_), channel_id=1, source_target_pairs={{0,8},{1,9},{2,10},{3,11},{4,12},{5,13},{6,14},{7,15},{8,0},{9,1},... | collective-permute-start | bytes 294920 | tf_op jit(solution)/shard_map/ppermute | solution.py:338
  54.4 1.4 %collective-permute-start.15 = (f32[64,64]{1,0:T(8,128)S(1)}, f32[64,64]{1,0:T(8,128)S(1)}, u32[]{:S(2)}, u32[]{:S(2)}) collective-permute-start(f32[64,64]{1,0:T(8,128)S(1)} %factor.3.inverse), channel_id=1, source_target_pairs={{0,8},{1,9},{2,10},{3,11},{4,12},{5,13},{6,14},{7,15},{8,0},{9,1},... | collective-permute-start | bytes 49160 | tf_op jit(solution)/shard_map/ppermute | solution.py:338

commit v3 on v2

--- a/solution.py
+++ b/solution.py
@@ -44,7 +44,8 @@
 
 
 def left_kernel(block, jobs, code, grad, error, basis, *refs):
-    outs, (grads, errors, factors, sems) = refs[:-4], refs[-4:]
+    *outs, late_error, late_grad, late_basis = refs[:-4]
+    grads, errors, factors, sems = refs[-4:]
     rank = basis.shape[1]
     copies = [pltpu.make_async_copy(basis, factors, sems.at[2, 0])]
     copies[0].start()
@@ -67,7 +68,16 @@
 
     for i in range(DEPTH):
         begin_block(i)
+    which, _, end = jobs[-1]
+    w, i, rest = bit(code, which), len(blocks), pl.ds(end, late_grad.shape[0])
+    late = (
+        pltpu.make_async_copy(error.at[0, w, rest], late_error, sems.at[0, i]),
+        pltpu.make_async_copy(grad.at[0, w, rest], late_grad, sems.at[1, i]),
+    )
+    for copy in late:
+        copy.start()
     copies[0].wait()
+    late_basis[...] = factors[w]
     cuts = []
     for which, _, _ in jobs:
         top, rest = split(factors[bit(code, which)])
@@ -84,29 +94,65 @@
         low[source] = lower
         both = dot(cut, upper, NT)
         left[:, source] = both[:rank] + both[rank:] + dot(top, lower, NT)
+    for copy in late:
+        copy.wait()
+
+
+def late_kernel(begin, error, grad, basis, _high, _low, _left, high, low, left):
+    rank, rows = left.shape
+    part = slice(begin, rows)
+    top, rest = split(basis[...])
+    upper, lower = split(grad[...].astype(F32) + error[...])
+    high[part] = upper
+    low[part] = lower
+    both = dot(jnp.concatenate([top, rest], axis=0), upper, NT)
+    left[:, part] = both[:rank] + both[rank:] + dot(top, lower, NT)
+
+
+def late_of(begin, error, grad, basis, high, low, left):
+    rows, cols = high.shape
+    rank = left.shape[0]
+    return pl.pallas_call(
+        functools.partial(late_kernel, begin),
+        name="late",
+        in_specs=[VMEM] * 6,
+        out_specs=[VMEM] * 3,
+        out_shape=[
+            shape_of(rows, cols, dtype=BF16),
+            shape_of(rows, cols, dtype=BF16),
+            shape_of(rank, rows),
+        ],
+        input_output_aliases={3: 0, 4: 1, 5: 2},
+        compiler_params=params(8),
+        cost_estimate=pl.CostEstimate(
+            flops=6 * (rows - begin) * cols * rank, bytes_accessed=8 * rows * cols, transcendentals=0
+        ),
+    )(error, grad, basis, high, low, left)
 
 
 def left_of(jobs, code, grad, error, basis):
     _, _, rows, cols = grad.shape
     rank = basis.shape[1]
-    block = min(rows, LEFT_ROWS)
+    block = min(rows // 2, LEFT_ROWS)
+    late = rows - jobs[-1][2]
     total = sum(end - begin for _, begin, end in jobs)
     return pl.pallas_call(
         functools.partial(left_kernel, block, jobs),
         name="left",
         in_specs=[SMEM, ANY, ANY, ANY],
-        out_specs=[VMEM] * (3 * len(jobs)),
+        out_specs=[VMEM] * (3 * len(jobs) + 3),
         out_shape=[
             shape_of(rows, cols, dtype=BF16),
             shape_of(rows, cols, dtype=BF16),
             shape_of(rank, rows),
         ]
-        * len(jobs),
+        * len(jobs)
+        + [shape_of(late, cols), shape_of(late, cols, dtype=BF16), shape_of(rank, cols)],
         scratch_shapes=[
             pltpu.VMEM((total, cols), BF16),
             pltpu.VMEM((total, cols), F32),
             pltpu.VMEM(basis.shape, F32),
-            pltpu.SemaphoreType.DMA((3, total // block)),
+            pltpu.SemaphoreType.DMA((3, total // block + 1)),
         ],
         compiler_params=params(24),
         cost_estimate=pl.CostEstimate(
@@ -360,9 +406,13 @@
     rank = basis.shape[1]
     rows, cols = grad_kv.shape[2:]
 
-    jobs = (theirs, 0, rows), (mine, 0, rows)
-    high_t, low_t, left_t, high_m, low_m, left_m = left_of(jobs, code, grad_kv, error_kv, basis)
+    ahead = rows // 2
+    jobs = (theirs, 0, rows), (mine, 0, ahead)
+    high_t, low_t, left_t, high_m, low_m, left_m, *late = left_of(
+        jobs, code, grad_kv, error_kv, basis
+    )
     arriving = core(left_t)
+    high_m, low_m, left_m = late_of(ahead, *late, high_m, low_m, left_m)
     left_m = left_m + arriving
     for step in r:
         left_m = left_m + swap(left_m, step)

time: 61.3 us -> 60.4 us (0.985)
  waiting for transfers between devices: 19 us -> 18.1 us
    pallas_call x1, Pallas kernels: 5.8 us -> 4.88 us  [left_of(): pl.pallas_call(functools.partial(left_kernel, block, jobs), name='left',...]
    pallas_call x0 -> x1, Pallas kernels: none -> 0.9 us  [late_of(): pl.pallas_call(functools.partial(late_kernel, begin), name='late', in_spe...]
    ppermute x18, waiting for transfers between devices: 19 us -> 18.1 us  [swap(): return lax.ppermute(value, AXES, pairs)]
  transfers between devices with their start and end apart: 18 -> 18, of which waited for: 12 -> 12; matrix products, arithmetic and copies ran while one was open for 0% -> 0% of each run, Pallas kernels for 11% -> 13%
where the time goes in v3:
time: 60.4 us; the launch traced here: 60.2 us
  starting transfers between devices  22.7 us (38%)
  Pallas kernels  18.4 us (30%)
  waiting for transfers between devices  18.1 us (30%)
  between operations  0.82 us (1%)
    ppermute x18, starting transfers between devices, swap(): return lax.ppermute(value, AXES, pairs)  22.7 us
    ppermute x18, waiting for transfers between devices, swap(): return lax.ppermute(value, AXES, pairs)  18.1 us
    pallas_call x1, Pallas kernels, final_of(): pl.pallas_call(functools.partial(final_kernel, block, scale, keeps), name...  5.28 us
    pallas_call x1, Pallas kernels, left_of(): pl.pallas_call(functools.partial(left_kernel, block, jobs), name='left',...  4.88 us
    pallas_call x2, Pallas kernels, factor_of(): pl.pallas_call(kernel, name='factor', in_specs=[VMEM], out_specs=VMEM, ou...  4.35 us
    pallas_call x3, Pallas kernels, right_of(): pl.pallas_call(functools.partial(right_kernel, [start for start, _ in col...  2.13 us
  transfers between devices with their start and end apart: 18, of which 12 were waited for; matrix products, arithmetic and copies ran while one was open for 0% of the time, Pallas kernels for 13%

profile of v3, /device:TPU:0, one launch (start us, length us, event | category | flops | bytes accessed | tf_op | source)
XLA Modules:
  0.0 60.2 jit_solution(1465981304765204764)
XLA Ops:
  0.6 4.9 %left.1 = (bf16[1024,1024]{1,0:T(8,128)(2,1)S(1)}, bf16[1024,1024]{1,0:T(8,128)(2,1)S(1)}, f32[64,1024]{1,0:T(8,128)S(1)}, bf16[1024,1024]{1,0:T(8,128)(2,1)S(1)...) custom-call(s32[1]{0:T(128)} %bitcast.code, ...), custom_call_target="tpu_custom_call" | custom-call | flops 603979776 | bytes 15728640 | tf_op jit(solution)/shard_map/left/pallas_call | solution.py:139
  5.5 0.6 collective-permute-start
  6.1 0.9 %late.1 = (bf16[1024,1024]{1,0:T(8,128)(2,1)S(1)}, bf16[1024,1024]{1,0:T(8,128)(2,1)S(1)}, f32[64,1024]{1,0:T(8,128)S(1)}) custom-call(f32[512,1024]{1,0:T(8,128)S(1)} %get-tuple-element.24.error, bf16[512,1024]{1,0:T(8,128)(2,1)S(1)} %get-tuple-element.25.grad, ...), custom_call_target="tpu_custom_call", output_to_operand_aliasing={{0}: (3, {}), {1}: (4, {}), {2}: (5, {})} | custom-call | flops 201326592 | bytes 8388608 | tf_op jit(solution)/shard_map/late/pallas_call | solution.py:115
  7.0 0.3 collective-permute-done
  7.3 3.0 %collective-permute-start.1 = (f32[64,1024]{1,0:T(8,128)S(1)}, f32[64,1024]{1,0:T(8,128)S(1)}, u32[]{:S(2)}, u32[]{:S(2)}) collective-permute-start(f32[64,1024]{1,0:T(8,128)S(1)} %add.48), channel_id=1, source_target_pairs={{0,16},{1,17},{2,18},{3,19},{4,20},{5,21},{6,22},{7,23},{8,24},{9,... | collective-permute-start | bytes 786440 | tf_op jit(solution)/shard_map/ppermute | solution.py:384
  10.2 6.6 %collective-permute-done.1 = f32[64,1024]{1,0:T(8,128)S(1)} collective-permute-done((f32[64,1024]{1,0:T(8,128)S(1)}, f32[64,1024]{1,0:T(8,128)S(1)}, u32[]{:S(2)}, u32[]{:S(2)}) %collective-permute-start.1) | collective-permute-done | bytes 262176 | tf_op jit(solution)/shard_map/ppermute | solution.py:384
  16.9 0.1 collective-permute-start.2
  17.0 1.5 %collective-permute-done.2.left.refs_6_ = f32[64,1024]{1,0:T(8,128)S(1)} collective-permute-done((f32[64,1024]{1,0:T(8,128)S(1)}, f32[64,1024]{1,0:T(8,128)S(1)}, u32[]{:S(2)}, u32[]{:S(2)}) %collective-permute-start.2) | collective-permute-done | bytes 262176 | tf_op jit(solution)/shard_map/ppermute | solution.py:384
  18.5 0.4 right.4
  18.9 0.2 collective-permute-start.3
  19.1 1.1 %right.3 = (f32[64,384]{1,0:T(8,128)S(1)}, f32[64,640]{1,0:T(8,128)S(1)}, f32[32,128]{1,0:T(8,128)S(1)}) custom-call(s32[1]{0:T(128)} %bitcast.code, f32[64,1024]{1,0:T(8,128)S(1)} %add_multiply_fusion.left, bf16[1024,1024]{1,0:T(8,128)(2,1)S(1)} %get-tuple-element.32.high.refs_3_, bf16[1024,1024]{1,0:T(8,128)(2,1)S(1)} %get-tuple-element.33.low.refs_4_), custom_call_target="tpu_custom_call" | custom-call | flops 402653184 | bytes 4194304 | tf_op jit(solution)/shard_map/right/pallas_call | solution.py:195
  20.2 0.6 %right.5 = f32[64,640]{1,0:T(8,128)S(1)} custom-call(s32[1]{0:T(128)} %bitcast.code, f32[64,1024]{1,0:T(8,128)S(1)} %collective-permute-done.2.left.refs_6_, bf16[1024,1024]{1,0:T(8,128)(2,1)S(1)} %get-tuple-element.35.high.refs_7_, bf16[1024,1024]{1,0:T(8,128)(2,1)S(1)} %get-tuple-element.36.low.refs_8_), custom_call_target="tpu_custom_call" | custom-call | flops 251658240 | bytes 2621440 | tf_op jit(solution)/shard_map/right/pallas_call | solution.py:195
  20.8 0.4 collective-permute-start.9
  21.3 0.0 collective-permute-done.3
  21.3 1.0 %collective-permute-done.9 = f32[64,640]{1,0:T(8,128)S(1)} collective-permute-done((f32[64,640]{1,0:T(8,128)S(1)}, f32[64,640]{1,0:T(8,128)S(1)}, u32[]{:S(2)}, u32[]{:S(2)}) %collective-permute-start.9) | collective-permute-done | bytes 163872 | tf_op jit(solution)/shard_map/ppermute | solution.py:384
  22.3 1.8 %collective-permute-start.10 = (f32[32,640]{1,0:T(8,128)S(1)}, f32[32,640]{1,0:T(8,128)S(1)}, u32[]{:S(2)}, u32[]{:S(2)}) collective-permute-start(f32[32,640]{1,0:T(8,128)S(1)} %slice.24), channel_id=1, source_target_pairs={{0,16},{1,17},{2,18},{3,19},{4,20},{5,21},{6,22},{7,23},{8,24},{9,... | collective-permute-start | bytes 245768 | tf_op jit(solution)/shard_map/ppermute | solution.py:384
  24.1 1.5 %collective-permute-start.4 = (f32[32,512]{1,0:T(8,128)S(1)}, f32[32,512]{1,0:T(8,128)S(1)}, u32[]{:S(2)}, u32[]{:S(2)}) collective-permute-start(f32[32,512]{1,0:T(8,128)S(1)} %pad_maximum_fusion.2), channel_id=1, source_target_pairs={{0,1},{1,0},{2,3},{3,2},{4,5},{5,4},{6,7},{7,6},{8,9},{9,8},{10,11... | collective-permute-start | bytes 196616 | tf_op jit(solution)/shard_map/ppermute | solution.py:384
  25.6 1.5 %collective-permute-done.10 = f32[32,640]{1,0:T(8,128)S(1)} collective-permute-done((f32[32,640]{1,0:T(8,128)S(1)}, f32[32,640]{1,0:T(8,128)S(1)}, u32[]{:S(2)}, u32[]{:S(2)}) %collective-permute-start.10) | collective-permute-done | bytes 81952 | tf_op jit(solution)/shard_map/ppermute | solution.py:384
  27.1 1.8 %collective-permute-start.11 = (f32[32,640]{1,0:T(8,128)S(1)}, f32[32,640]{1,0:T(8,128)S(1)}, u32[]{:S(2)}, u32[]{:S(2)}) collective-permute-start(f32[32,640]{1,0:T(8,128)S(1)} %slice_add_fusion), channel_id=1, source_target_pairs={{0,1},{1,0},{2,3},{3,2},{4,5},{5,4},{6,7},{7,6},{8,9},{9,8},{10,11... | collective-permute-start | bytes 245768 | tf_op jit(solution)/shard_map/ppermute | solution.py:384
  28.9 0.0 collective-permute-done.4
  28.9 1.6 %collective-permute-start.5 = (f32[32,512]{1,0:T(8,128)S(1)}, f32[32,512]{1,0:T(8,128)S(1)}, u32[]{:S(2)}, u32[]{:S(2)}) collective-permute-start(f32[32,512]{1,0:T(8,128)S(1)} %fusion), channel_id=1, source_target_pairs={{0,2},{1,3},{2,0},{3,1},{4,6},{5,7},{6,4},{7,5},{8,10},{9,11},{10,... | collective-permute-start | bytes 196616 | tf_op jit(solution)/shard_map/ppermute | solution.py:384
  30.6 1.1 %collective-permute-done.11 = f32[32,640]{1,0:T(8,128)S(1)} collective-permute-done((f32[32,640]{1,0:T(8,128)S(1)}, f32[32,640]{1,0:T(8,128)S(1)}, u32[]{:S(2)}, u32[]{:S(2)}) %collective-permute-start.11) | collective-permute-done | bytes 81952 | tf_op jit(solution)/shard_map/ppermute | solution.py:384
  31.6 1.8 %collective-permute-start.12 = (f32[32,640]{1,0:T(8,128)S(1)}, f32[32,640]{1,0:T(8,128)S(1)}, u32[]{:S(2)}, u32[]{:S(2)}) collective-permute-start(f32[32,640]{1,0:T(8,128)S(1)} %add.57), channel_id=1, source_target_pairs={{0,2},{1,3},{2,0},{3,1},{4,6},{5,7},{6,4},{7,5},{8,10},{9,11},{10,... | collective-permute-start | bytes 245768 | tf_op jit(solution)/shard_map/ppermute | solution.py:384
  33.5 0.3 collective-permute-done.5
  33.8 2.5 %collective-permute-start.6 = (f32[32,512]{1,0:T(8,128)S(1)}, f32[32,512]{1,0:T(8,128)S(1)}, u32[]{:S(2)}, u32[]{:S(2)}) collective-permute-start(f32[32,512]{1,0:T(8,128)S(1)} %add.52), channel_id=1, source_target_pairs={{0,4},{1,5},{2,6},{3,7},{4,0},{5,1},{6,2},{7,3},{8,12},{9,13},{10,... | collective-permute-start | bytes 196616 | tf_op jit(solution)/shard_map/ppermute | solution.py:384
  36.3 0.5 collective-permute-done.12
  36.8 2.2 %collective-permute-start.13 = (f32[32,640]{1,0:T(8,128)S(1)}, f32[32,640]{1,0:T(8,128)S(1)}, u32[]{:S(2)}, u32[]{:S(2)}) collective-permute-start(f32[32,640]{1,0:T(8,128)S(1)} %add.58), channel_id=1, source_target_pairs={{0,4},{1,5},{2,6},{3,7},{4,0},{5,1},{6,2},{7,3},{8,12},{9,13},{10,... | collective-permute-start | bytes 245768 | tf_op jit(solution)/shard_map/ppermute | solution.py:384
  39.0 1.7 %collective-permute-done.6 = f32[32,512]{1,0:T(8,128)S(1)} collective-permute-done((f32[32,512]{1,0:T(8,128)S(1)}, f32[32,512]{1,0:T(8,128)S(1)}, u32[]{:S(2)}, u32[]{:S(2)}) %collective-permute-start.6) | collective-permute-done | bytes 65568 | tf_op jit(solution)/shard_map/ppermute | solution.py:384
  40.8 1.6 %collective-permute-start.7 = (f32[32,384]{1,0:T(8,128)S(1)}, f32[32,384]{1,0:T(8,128)S(1)}, u32[]{:S(2)}, u32[]{:S(2)}) collective-permute-start(f32[32,384]{1,0:T(8,128)S(1)} %slice.22), channel_id=1, source_target_pairs={{0,16},{1,17},{2,18},{3,19},{4,20},{5,21},{6,22},{7,23},{8,24},{9,... | collective-permute-start | bytes 147464 | tf_op jit(solution)/shard_map/ppermute | solution.py:384
  42.4 0.0 collective-permute-done.13
  42.4 1.4 %collective-permute-start.14 = (f32[32,640]{1,0:T(8,128)S(1)}, f32[32,640]{1,0:T(8,128)S(1)}, u32[]{:S(2)}, u32[]{:S(2)}) collective-permute-start(f32[32,640]{1,0:T(8,128)S(1)} %add.59), channel_id=1, source_target_pairs={{0,16},{1,17},{2,18},{3,19},{4,20},{5,21},{6,22},{7,23},{8,24},{9,... | collective-permute-start | bytes 245768 | tf_op jit(solution)/shard_map/ppermute | solution.py:384
  43.8 1.1 %collective-permute-done.7 = f32[32,384]{1,0:T(8,128)S(1)} collective-permute-done((f32[32,384]{1,0:T(8,128)S(1)}, f32[32,384]{1,0:T(8,128)S(1)}, u32[]{:S(2)}, u32[]{:S(2)}) %collective-permute-start.7) | collective-permute-done | bytes 49184 | tf_op jit(solution)/shard_map/ppermute | solution.py:384
  44.9 1.5 %collective-permute-start.8 = (f32[32,384]{1,0:T(8,128)S(1)}, f32[32,384]{1,0:T(8,128)S(1)}, u32[]{:S(2)}, u32[]{:S(2)}) collective-permute-start(f32[32,384]{1,0:T(8,128)S(1)} %slice_add_fusion.1), channel_id=1, source_target_pairs={{0,1},{1,0},{2,3},{3,2},{4,5},{5,4},{6,7},{7,6},{8,9},{9,8},{10,11... | collective-permute-start | bytes 147464 | tf_op jit(solution)/shard_map/ppermute | solution.py:384
  46.4 0.4 collective-permute-done.14
  46.9 0.1 collective-permute-start.17
  47.0 2.1 %collective-permute-done.8 = f32[32,384]{1,0:T(8,128)S(1)} collective-permute-done((f32[32,384]{1,0:T(8,128)S(1)}, f32[32,384]{1,0:T(8,128)S(1)}, u32[]{:S(2)}, u32[]{:S(2)}) %collective-permute-start.8) | collective-permute-done | bytes 49184 | tf_op jit(solution)/shard_map/ppermute | solution.py:384
  49.1 0.1 collective-permute-start.16
  49.2 2.3 %factor.2.work = f32[64,128]{1,0:T(8,128)S(1)} custom-call(f32[32,512]{1,0:T(8,128)S(1)} %add.53.packed), custom_call_target="tpu_custom_call" | custom-call | flops 524288 | bytes 32768 | tf_op jit(solution)/shard_map/factor/pallas_call | solution.py:257
  51.4 2.1 %factor.3.inverse = f32[64,64]{1,0:T(8,128)S(1)} custom-call(f32[64,128]{1,0:T(8,128)S(1)} %factor.2.work), custom_call_target="tpu_custom_call" | custom-call | flops 524288 | bytes 32768 | tf_op jit(solution)/shard_map/factor/pallas_call | solution.py:257
  53.5 0.5 collective-permute-start.15
  54.0 0.9 %prepare.1 = (f32[64,1024]{1,0:T(8,128)S(1)}, bf16[192,1024]{1,0:T(8,128)(2,1)S(1)}, bf16[1024,192]{1,0:T(8,128)(2,1)S(1)}) custom-call(s32[1]{0:T(128)} %bitcast.code, f32[64,64]{1,0:T(8,128)S(1)} %factor.3.inverse, f32[64,1024]{1,0:T(8,128)S(1)} %add_multiply_fusion.left, f32[64,384]{1,0:T(8,128)S(1)} %pad_maximum_fusion.1.refs_0_, ...), custom_call_target="tpu_custom_call" | custom-call | flops 100663296 | bytes 1310720 | tf_op jit(solution)/shard_map/prepare/pallas_call | solution.py:291
  54.9 0.0 collective-permute-done.15.refs_5_
  54.9 0.0 collective-permute-done.16.refs_9_
  54.9 0.0 collective-permute-done.17.refs_10_
  54.9 5.3 %final.1 = (bf16[2,1024,1024]{2,1,0:T(8,128)(2,1)}, f32[1,2,1024,1024]{3,2,1,0:T(8,128)}, f32[2,64,1024]{2,1,0:T(8,128)}) custom-call(s32[1]{0:T(128)} %bitcast.code, f32[64,1024]{1,0:T(8,128)S(1)} %get-tuple-element.39.refs_0_, bf16[192,1024]{1,0:T(8,128)(2,1)S(1)} %get-tuple-element.40.refs_1_, bf16[1024,192]{1,0:T(8,128)(2,1)S(1)} %get-tuple-element.41.refs_2_, ...), custom_call_target="tpu_custom_call" | custom-call | flops 805306368 | bytes 20971520 | tf_op jit(solution)/shard_map/final/pallas_call | solution.py:343
  (18 shorter events, 0.2 us)
Async XLA Ops:
  5.5 1.7 %collective-permute-start = (f32[64,1024]{1,0:T(8,128)S(1)}, f32[64,1024]{1,0:T(8,128)S(1)}, u32[]{:S(2)}, u32[]{:S(2)}) collective-permute-start(f32[64,1024]{1,0:T(8,128)S(1)} %get-tuple-element.31), channel_id=1, source_target_pairs={{0,8},{1,9},{2,10},{3,11},{4,12},{5,13},{6,14},{7,15},{8,0},{9,1},... | collective-permute-start | bytes 786440 | tf_op jit(solution)/shard_map/ppermute | solution.py:384
  7.3 9.6 %collective-permute-start.1 = (f32[64,1024]{1,0:T(8,128)S(1)}, f32[64,1024]{1,0:T(8,128)S(1)}, u32[]{:S(2)}, u32[]{:S(2)}) collective-permute-start(f32[64,1024]{1,0:T(8,128)S(1)} %add.48), channel_id=1, source_target_pairs={{0,16},{1,17},{2,18},{3,19},{4,20},{5,21},{6,22},{7,23},{8,24},{9,... | collective-permute-start | bytes 786440 | tf_op jit(solution)/shard_map/ppermute | solution.py:384
  16.9 1.6 %collective-permute-start.2 = (f32[64,1024]{1,0:T(8,128)S(1)}, f32[64,1024]{1,0:T(8,128)S(1)}, u32[]{:S(2)}, u32[]{:S(2)}) collective-permute-start(f32[64,1024]{1,0:T(8,128)S(1)} %add_multiply_fusion.left), channel_id=1, source_target_pairs={{0,8},{1,9},{2,10},{3,11},{4,12},{5,13},{6,14},{7,15},{8,0},{9,1},... | collective-permute-start | bytes 786440 | tf_op jit(solution)/shard_map/ppermute | solution.py:384
  18.9 2.4 %collective-permute-start.3 = (f32[64,384]{1,0:T(8,128)S(1)}, f32[64,384]{1,0:T(8,128)S(1)}, u32[]{:S(2)}, u32[]{:S(2)}) collective-permute-start(f32[64,384]{1,0:T(8,128)S(1)} %right.4), channel_id=1, source_target_pairs={{0,8},{1,9},{2,10},{3,11},{4,12},{5,13},{6,14},{7,15},{8,0},{9,1},... | collective-permute-start | bytes 294920 | tf_op jit(solution)/shard_map/ppermute | solution.py:384
  20.8 1.5 %collective-permute-start.9 = (f32[64,640]{1,0:T(8,128)S(1)}, f32[64,640]{1,0:T(8,128)S(1)}, u32[]{:S(2)}, u32[]{:S(2)}) collective-permute-start(f32[64,640]{1,0:T(8,128)S(1)} %right.5), channel_id=1, source_target_pairs={{0,8},{1,9},{2,10},{3,11},{4,12},{5,13},{6,14},{7,15},{8,0},{9,1},... | collective-permute-start | bytes 491528 | tf_op jit(solution)/shard_map/ppermute | solution.py:384
  22.3 4.8 %collective-permute-start.10 = (f32[32,640]{1,0:T(8,128)S(1)}, f32[32,640]{1,0:T(8,128)S(1)}, u32[]{:S(2)}, u32[]{:S(2)}) collective-permute-start(f32[32,640]{1,0:T(8,128)S(1)} %slice.24), channel_id=1, source_target_pairs={{0,16},{1,17},{2,18},{3,19},{4,20},{5,21},{6,22},{7,23},{8,24},{9,... | collective-permute-start | bytes 245768 | tf_op jit(solution)/shard_map/ppermute | solution.py:384
  24.1 4.8 %collective-permute-start.4 = (f32[32,512]{1,0:T(8,128)S(1)}, f32[32,512]{1,0:T(8,128)S(1)}, u32[]{:S(2)}, u32[]{:S(2)}) collective-permute-start(f32[32,512]{1,0:T(8,128)S(1)} %pad_maximum_fusion.2), channel_id=1, source_target_pairs={{0,1},{1,0},{2,3},{3,2},{4,5},{5,4},{6,7},{7,6},{8,9},{9,8},{10,11... | collective-permute-start | bytes 196616 | tf_op jit(solution)/shard_map/ppermute | solution.py:384
  27.1 4.5 %collective-permute-start.11 = (f32[32,640]{1,0:T(8,128)S(1)}, f32[32,640]{1,0:T(8,128)S(1)}, u32[]{:S(2)}, u32[]{:S(2)}) collective-permute-start(f32[32,640]{1,0:T(8,128)S(1)} %slice_add_fusion), channel_id=1, source_target_pairs={{0,1},{1,0},{2,3},{3,2},{4,5},{5,4},{6,7},{7,6},{8,9},{9,8},{10,11... | collective-permute-start | bytes 245768 | tf_op jit(solution)/shard_map/ppermute | solution.py:384
  28.9 4.9 %collective-permute-start.5 = (f32[32,512]{1,0:T(8,128)S(1)}, f32[32,512]{1,0:T(8,128)S(1)}, u32[]{:S(2)}, u32[]{:S(2)}) collective-permute-start(f32[32,512]{1,0:T(8,128)S(1)} %fusion), channel_id=1, source_target_pairs={{0,2},{1,3},{2,0},{3,1},{4,6},{5,7},{6,4},{7,5},{8,10},{9,11},{10,... | collective-permute-start | bytes 196616 | tf_op jit(solution)/shard_map/ppermute | solution.py:384
  31.6 5.1 %collective-permute-start.12 = (f32[32,640]{1,0:T(8,128)S(1)}, f32[32,640]{1,0:T(8,128)S(1)}, u32[]{:S(2)}, u32[]{:S(2)}) collective-permute-start(f32[32,640]{1,0:T(8,128)S(1)} %add.57), channel_id=1, source_target_pairs={{0,2},{1,3},{2,0},{3,1},{4,6},{5,7},{6,4},{7,5},{8,10},{9,11},{10,... | collective-permute-start | bytes 245768 | tf_op jit(solution)/shard_map/ppermute | solution.py:384
  33.8 7.0 %collective-permute-start.6 = (f32[32,512]{1,0:T(8,128)S(1)}, f32[32,512]{1,0:T(8,128)S(1)}, u32[]{:S(2)}, u32[]{:S(2)}) collective-permute-start(f32[32,512]{1,0:T(8,128)S(1)} %add.52), channel_id=1, source_target_pairs={{0,4},{1,5},{2,6},{3,7},{4,0},{5,1},{6,2},{7,3},{8,12},{9,13},{10,... | collective-permute-start | bytes 196616 | tf_op jit(solution)/shard_map/ppermute | solution.py:384
  36.8 5.6 %collective-permute-start.13 = (f32[32,640]{1,0:T(8,128)S(1)}, f32[32,640]{1,0:T(8,128)S(1)}, u32[]{:S(2)}, u32[]{:S(2)}) collective-permute-start(f32[32,640]{1,0:T(8,128)S(1)} %add.58), channel_id=1, source_target_pairs={{0,4},{1,5},{2,6},{3,7},{4,0},{5,1},{6,2},{7,3},{8,12},{9,13},{10,... | collective-permute-start | bytes 245768 | tf_op jit(solution)/shard_map/ppermute | solution.py:384
  40.8 4.2 %collective-permute-start.7 = (f32[32,384]{1,0:T(8,128)S(1)}, f32[32,384]{1,0:T(8,128)S(1)}, u32[]{:S(2)}, u32[]{:S(2)}) collective-permute-start(f32[32,384]{1,0:T(8,128)S(1)} %slice.22), channel_id=1, source_target_pairs={{0,16},{1,17},{2,18},{3,19},{4,20},{5,21},{6,22},{7,23},{8,24},{9,... | collective-permute-start | bytes 147464 | tf_op jit(solution)/shard_map/ppermute | solution.py:384
  42.4 4.5 %collective-permute-start.14 = (f32[32,640]{1,0:T(8,128)S(1)}, f32[32,640]{1,0:T(8,128)S(1)}, u32[]{:S(2)}, u32[]{:S(2)}) collective-permute-start(f32[32,640]{1,0:T(8,128)S(1)} %add.59), channel_id=1, source_target_pairs={{0,16},{1,17},{2,18},{3,19},{4,20},{5,21},{6,22},{7,23},{8,24},{9,... | collective-permute-start | bytes 245768 | tf_op jit(solution)/shard_map/ppermute | solution.py:384
  44.9 4.2 %collective-permute-start.8 = (f32[32,384]{1,0:T(8,128)S(1)}, f32[32,384]{1,0:T(8,128)S(1)}, u32[]{:S(2)}, u32[]{:S(2)}) collective-permute-start(f32[32,384]{1,0:T(8,128)S(1)} %slice_add_fusion.1), channel_id=1, source_target_pairs={{0,1},{1,0},{2,3},{3,2},{4,5},{5,4},{6,7},{7,6},{8,9},{9,8},{10,11... | collective-permute-start | bytes 147464 | tf_op jit(solution)/shard_map/ppermute | solution.py:384
  46.9 8.0 %collective-permute-start.17 = (f32[64,640]{1,0:T(8,128)S(1)}, f32[64,640]{1,0:T(8,128)S(1)}, u32[]{:S(2)}, u32[]{:S(2)}) collective-permute-start(f32[64,640]{1,0:T(8,128)S(1)} %pad_maximum_fusion.refs_1_), channel_id=1, source_target_pairs={{0,8},{1,9},{2,10},{3,11},{4,12},{5,13},{6,14},{7,15},{8,0},{9,1},... | collective-permute-start | bytes 491528 | tf_op jit(solution)/shard_map/ppermute | solution.py:384
  49.1 5.8 %collective-permute-start.16 = (f32[64,384]{1,0:T(8,128)S(1)}, f32[64,384]{1,0:T(8,128)S(1)}, u32[]{:S(2)}, u32[]{:S(2)}) collective-permute-start(f32[64,384]{1,0:T(8,128)S(1)} %pad_maximum_fusion.1.refs_0_), channel_id=1, source_target_pairs={{0,8},{1,9},{2,10},{3,11},{4,12},{5,13},{6,14},{7,15},{8,0},{9,1},... | collective-permute-start | bytes 294920 | tf_op jit(solution)/shard_map/ppermute | solution.py:384
  53.5 1.4 %collective-permute-start.15 = (f32[64,64]{1,0:T(8,128)S(1)}, f32[64,64]{1,0:T(8,128)S(1)}, u32[]{:S(2)}, u32[]{:S(2)}) collective-permute-start(f32[64,64]{1,0:T(8,128)S(1)} %factor.3.inverse), channel_id=1, source_target_pairs={{0,8},{1,9},{2,10},{3,11},{4,12},{5,13},{6,14},{7,15},{8,0},{9,1},... | collective-permute-start | bytes 49160 | tf_op jit(solution)/shard_map/ppermute | solution.py:384
